TPU v7x, 32 devices: a whole 2x2x4 slice. The times are simulated.
32 devices in a mesh: seq: 2 (over x), shard: 16 (over z, y, core).
Axes of the slice: x: 2, y: 2, z: 4, core: 2. Of those that a mesh axis runs over, the one named last changes fastest.
Arguments:
- hidden: bfloat16 [2, 32, 1024, 768], P(None, 'shard', 'seq'), may hold values from -6 to 6
- cotangent: bfloat16 [2, 32, 1024, 768], P(None, 'shard', 'seq'), may hold values from -6 to 6
- segments: int32 [2, 32, 1024], P(None, 'shard', 'seq'), may hold values from 0 to 3, never falling along the last dimension, each value on 1 to 512 neighbouring positions
- w_qkv: bfloat16 [768, 2304], P('shard'), may hold values from -0.21875 to 0.21875
- bias_q: bfloat16 [768], P('shard'), may hold values from -3 to 3
- bias_v: bfloat16 [768], P('shard'), may hold values from -0.5 to 0.5
- w_out: bfloat16 [768, 768], P('shard'), may hold values from -1.25 to 1.25
- bias_out: bfloat16 [768], P('shard'), may hold values from -3 to 3
- norm1_gain: bfloat16 [768], P('shard'), may hold values from 0.5 to 1.5
- norm1_bias: bfloat16 [768], P('shard'), may hold values from -3 to 3
- w_up: bfloat16 [768, 3072], P('shard'), may hold values from -0.21875 to 0.21875
- bias_up: bfloat16 [3072], P('shard'), may hold values from -3 to 3
- w_down: bfloat16 [3072, 768], P('shard'), may hold values from -0.109375 to 0.109375
- bias_down: bfloat16 [768], P('shard'), may hold values from -3 to 3
- norm2_gain: bfloat16 [768], P('shard'), may hold values from 0.5 to 1.5
- norm2_bias: bfloat16 [768], P('shard'), may hold values from -3 to 3
Outputs:
- layer_out: bfloat16 [2, 32, 1024, 768], P(None, 'shard', 'seq')
- grad_hidden: bfloat16 [2, 32, 1024, 768], P(None, 'shard', 'seq')
- grad_w_qkv: float32 [768, 2304], P('shard')
- grad_bias_q: float32 [768], P('shard')
- grad_bias_v: float32 [768], P('shard')
- grad_w_out: float32 [768, 768], P('shard')
- grad_bias_out: float32 [768], P('shard')
- grad_norm1_gain: float32 [768], P('shard')
- grad_norm1_bias: float32 [768], P('shard')
- grad_w_up: float32 [768, 3072], P('shard')
- grad_bias_up: float32 [3072], P('shard')
- grad_w_down: float32 [3072, 768], P('shard')
- grad_bias_down: float32 [768], P('shard')
- grad_norm2_gain: float32 [768], P('shard')
- grad_norm2_bias: float32 [768], P('shard')
Inputs may be any that keep to these rules, and one draw needn't show every extreme that they name: `segments`: along each sequence of 1024 tokens the document numbers never fall; each of the 4 documents has 1 to 512 tokens, and one has exactly 512.
All inputs are finite; a program needn't handle non-finite values.
Results may differ from a plain program's by a relative error of at most 0.014.
Values may be sent and summed in bfloat16 or wider, within the bound.
No kernel may reach another device: no remote copies, remote signals or barrier semaphores. Data moves between devices by JAX's collectives and lax.ppermute only.
A program may use at most 256 MiB of HBM per device.

v0:
```python
import jax
import jax.numpy as jnp
from jax import lax
from jax.sharding import PartitionSpec as P

HD = 64


eps_norm = 1e-05
masked_score = -1e30


def shortened(array):
    return jax.tree.map(lambda a: a.astype(jnp.bfloat16) if a.dtype == jnp.float32 else a, array)


def norm_apply(resid, gain, offset):
    center = jnp.mean(resid, axis=-1, keepdims=True)
    deviate = resid - center
    spread = jnp.mean(deviate * deviate, axis=-1, keepdims=True)
    return deviate * lax.rsqrt(spread + eps_norm) * gain + offset


def gelu_exact(values):
    return jax.nn.gelu(values, approximate=False)


def split_heads(packed, head_width):
    seq_count, seq_length, columns = packed.shape
    return (
        packed.reshape(seq_count, seq_length, columns // head_width, head_width)
        .transpose(0, 2, 1, 3)
        .reshape(-1, seq_length, head_width)
    )


def join_heads(pieces, seq_count):
    count_all, seq_length, head_width = pieces.shape
    return (
        pieces.reshape(seq_count, count_all // seq_count, seq_length, head_width)
        .transpose(0, 2, 1, 3)
        .reshape(seq_count, seq_length, -1)
    )


def masked_scores(query_rows, key_head, doc_query, doc_keys, score_scale):
    scores = (
        jnp.einsum("qe,ke->qk", query_rows, key_head, preferred_element_type=jnp.float32)
        * score_scale
    )
    return jnp.where(doc_query[:, None] == doc_keys[None, :], scores, masked_score)


def attend_forward(queries, keys_heads, values_heads, doc_items, score_scale):

    def one_head(element):
        query_head, key_head, value_head, doc_row = element
        seq_length = query_head.shape[0]
        block_rows = min(seq_length, 512)
        context_parts = []
        lse_parts = []
        for row_start in range(0, seq_length, block_rows):
            query_rows = query_head[row_start : row_start + block_rows]
            scores = masked_scores(
                query_rows,
                key_head,
                doc_row[row_start : row_start + block_rows],
                doc_row,
                score_scale,
            )
            row_top = jnp.max(scores, axis=1, keepdims=True)
            raised = jnp.exp(scores - row_top)
            row_total = jnp.sum(raised, axis=1, keepdims=True)
            soft_probs = (raised / row_total).astype(jnp.bfloat16)
            context_parts.append(
                jnp.dot(soft_probs, value_head, preferred_element_type=jnp.float32)
            )
            lse_parts.append(row_top + jnp.log(row_total))
        return (jnp.concatenate(context_parts, axis=0), jnp.concatenate(lse_parts, axis=0))

    return lax.map(one_head, (queries, keys_heads, values_heads, doc_items))


def attend_backward(queries, keys_heads, values_heads, doc_items, grad_heads, lse_all, score_scale):

    def one_head(element):
        query_head, key_head, value_head, doc_row, grad_head, lse_head = element
        seq_length = query_head.shape[0]
        block_rows = min(seq_length, 512)
        grad_keys = jnp.zeros(key_head.shape, jnp.float32)
        grad_values = jnp.zeros(value_head.shape, jnp.float32)
        query_parts = []
        for row_start in range(0, seq_length, block_rows):
            query_rows = query_head[row_start : row_start + block_rows]
            grad_rows = grad_head[row_start : row_start + block_rows]
            scores = masked_scores(
                query_rows,
                key_head,
                doc_row[row_start : row_start + block_rows],
                doc_row,
                score_scale,
            )
            soft_probs = jnp.exp(scores - lse_head[row_start : row_start + block_rows])
            grad_values = grad_values + jnp.einsum(
                "qk,qe->ke",
                soft_probs.astype(jnp.bfloat16),
                grad_rows,
                preferred_element_type=jnp.float32,
            )
            grad_probs = jnp.einsum(
                "qe,ke->qk", grad_rows, value_head, preferred_element_type=jnp.float32
            )
            inner = jnp.sum(soft_probs * grad_probs, axis=1, keepdims=True)
            grad_scores = (soft_probs * (grad_probs - inner)).astype(jnp.bfloat16)
            query_parts.append(
                jnp.dot(grad_scores, key_head, preferred_element_type=jnp.float32) * score_scale
            )
            grad_keys = (
                grad_keys
                + jnp.einsum(
                    "qk,qe->ke", grad_scores, query_rows, preferred_element_type=jnp.float32
                )
                * score_scale
            )
        grad_queries = jnp.concatenate(query_parts, axis=0)
        return (
            grad_queries.astype(jnp.bfloat16),
            grad_keys.astype(jnp.bfloat16),
            grad_values.astype(jnp.bfloat16),
        )

    return lax.map(one_head, (queries, keys_heads, values_heads, doc_items, grad_heads, lse_all))


def local(
    hidden,
    cotangent,
    segments,
    w_qkv,
    bias_q,
    bias_v,
    w_out,
    bias_out,
    norm1_gain,
    norm1_bias,
    w_up,
    bias_up,
    w_down,
    bias_down,
    norm2_gain,
    norm2_bias,
):
    owned = (
        w_qkv,
        bias_q,
        bias_v,
        w_out,
        bias_out,
        norm1_gain,
        norm1_bias,
        w_up,
        bias_up,
        w_down,
        bias_down,
        norm2_gain,
        norm2_bias,
    )
    micro_count = hidden.shape[0]
    seq_count = hidden.shape[1]
    model_width = hidden.shape[3]
    score_scale = HD ** (-0.5)
    doc_full = lax.all_gather(segments, "seq", axis=2, tiled=True)
    stored = []
    outputs = []
    for micro_index in range(micro_count):
        params = (
            lax.all_gather(owned[0], "shard", axis=0, tiled=True),
            lax.all_gather(owned[1], "shard", axis=0, tiled=True),
            lax.all_gather(owned[2], "shard", axis=0, tiled=True),
            lax.all_gather(owned[3], "shard", axis=0, tiled=True),
            lax.all_gather(owned[4], "shard", axis=0, tiled=True),
            lax.all_gather(owned[5], "shard", axis=0, tiled=True),
            lax.all_gather(owned[6], "shard", axis=0, tiled=True),
            lax.all_gather(owned[7], "shard", axis=0, tiled=True),
            lax.all_gather(owned[8], "shard", axis=0, tiled=True),
            lax.all_gather(owned[9], "shard", axis=0, tiled=True),
            lax.all_gather(owned[10], "shard", axis=0, tiled=True),
            lax.all_gather(owned[11], "shard", axis=0, tiled=True),
            lax.all_gather(owned[12], "shard", axis=0, tiled=True),
        )
        (
            proj_weight,
            query_bias,
            value_bias,
            attn_weight,
            attn_bias,
            gain_first,
            shift_first,
            upper_weight,
            upper_bias,
            lower_weight,
            lower_bias,
            gain_second,
            shift_second,
        ) = params
        inputs = hidden[micro_index]
        offsets = jnp.concatenate([query_bias, jnp.zeros_like(query_bias), value_bias]).astype(
            jnp.float32
        )
        projected = (
            jnp.einsum("bld,de->ble", inputs, proj_weight, preferred_element_type=jnp.float32)
            + offsets
        ).astype(jnp.bfloat16)
        query_all, key_all, value_all = (
            lax.all_to_all(
                projected[:, :, :model_width], "seq", split_axis=2, concat_axis=1, tiled=True
            ),
            lax.all_to_all(
                projected[:, :, model_width : 2 * model_width],
                "seq",
                split_axis=2,
                concat_axis=1,
                tiled=True,
            ),
            lax.all_to_all(
                projected[:, :, 2 * model_width :], "seq", split_axis=2, concat_axis=1, tiled=True
            ),
        )
        heads_here = query_all.shape[2] // HD
        doc_items = jnp.repeat(doc_full[micro_index], heads_here, axis=0)
        queries = split_heads(query_all, HD)
        keys_heads = split_heads(key_all, HD)
        values_heads = split_heads(value_all, HD)
        context_heads, lse_all = attend_forward(
            queries, keys_heads, values_heads, doc_items, score_scale
        )
        context_full = join_heads(context_heads.astype(jnp.bfloat16), seq_count)
        context_local = lax.all_to_all(
            shortened(context_full), "seq", split_axis=1, concat_axis=2, tiled=True
        ).astype(context_full.dtype)
        attn_out = jnp.einsum(
            "bld,de->ble", context_local, attn_weight, preferred_element_type=jnp.float32
        ) + attn_bias.astype(jnp.float32)
        resid_first = inputs.astype(jnp.float32) + attn_out
        normed_first = norm_apply(
            resid_first, gain_first.astype(jnp.float32), shift_first.astype(jnp.float32)
        )
        normed_low = normed_first.astype(jnp.bfloat16)
        upper_pre = jnp.einsum(
            "bld,df->blf", normed_low, upper_weight, preferred_element_type=jnp.float32
        ) + upper_bias.astype(jnp.float32)
        activated = gelu_exact(upper_pre).astype(jnp.bfloat16)
        lower_out = jnp.einsum(
            "blf,fd->bld", activated, lower_weight, preferred_element_type=jnp.float32
        ) + lower_bias.astype(jnp.float32)
        resid_second = normed_first + lower_out
        outputs.append(
            norm_apply(
                resid_second, gain_second.astype(jnp.float32), shift_second.astype(jnp.float32)
            ).astype(jnp.bfloat16)
        )
        stored.append(
            (
                queries,
                keys_heads,
                values_heads,
                doc_items,
                lse_all,
                context_local,
                resid_first,
                normed_low,
                upper_pre,
                activated,
                resid_second,
            )
        )
    accum = None
    grads_in = []
    for micro_index in range(micro_count):
        params = (
            lax.all_gather(owned[0], "shard", axis=0, tiled=True),
            lax.all_gather(owned[1], "shard", axis=0, tiled=True),
            lax.all_gather(owned[2], "shard", axis=0, tiled=True),
            lax.all_gather(owned[3], "shard", axis=0, tiled=True),
            lax.all_gather(owned[4], "shard", axis=0, tiled=True),
            lax.all_gather(owned[5], "shard", axis=0, tiled=True),
            lax.all_gather(owned[6], "shard", axis=0, tiled=True),
            lax.all_gather(owned[7], "shard", axis=0, tiled=True),
            lax.all_gather(owned[8], "shard", axis=0, tiled=True),
            lax.all_gather(owned[9], "shard", axis=0, tiled=True),
            lax.all_gather(owned[10], "shard", axis=0, tiled=True),
            lax.all_gather(owned[11], "shard", axis=0, tiled=True),
            lax.all_gather(owned[12], "shard", axis=0, tiled=True),
        )
        (
            proj_weight,
            query_bias,
            value_bias,
            attn_weight,
            attn_bias,
            gain_first,
            shift_first,
            upper_weight,
            upper_bias,
            lower_weight,
            lower_bias,
            gain_second,
            shift_second,
        ) = params
        (
            queries,
            keys_heads,
            values_heads,
            doc_items,
            lse_all,
            context_local,
            resid_first,
            normed_low,
            upper_pre,
            activated,
            resid_second,
        ) = stored[micro_index]
        inputs = hidden[micro_index]
        upstream = cotangent[micro_index].astype(jnp.float32)
        unused_out, norm_pull = jax.vjp(
            norm_apply,
            resid_second,
            gain_second.astype(jnp.float32),
            shift_second.astype(jnp.float32),
        )
        grad_resid_two, grad_gain_two, grad_shift_two = norm_pull(upstream)
        grad_lower = grad_resid_two.astype(jnp.bfloat16)
        grad_lower_bias = jnp.sum(grad_lower.astype(jnp.float32), axis=(0, 1))
        grad_lower_weight = jnp.einsum(
            "blf,bld->fd", activated, grad_lower, preferred_element_type=jnp.float32
        )
        grad_activated = jnp.einsum(
            "bld,fd->blf", grad_lower, lower_weight, preferred_element_type=jnp.float32
        )
        unused_gelu, gelu_pull = jax.vjp(gelu_exact, upper_pre)
        grad_upper = gelu_pull(grad_activated)[0].astype(jnp.bfloat16)
        grad_upper_bias = jnp.sum(grad_upper.astype(jnp.float32), axis=(0, 1))
        grad_upper_weight = jnp.einsum(
            "bld,blf->df", normed_low, grad_upper, preferred_element_type=jnp.float32
        )
        grad_normed = grad_resid_two + jnp.einsum(
            "blf,df->bld", grad_upper, upper_weight, preferred_element_type=jnp.float32
        )
        unused_norm, first_pull = jax.vjp(
            norm_apply, resid_first, gain_first.astype(jnp.float32), shift_first.astype(jnp.float32)
        )
        grad_resid_one, grad_gain_one, grad_shift_one = first_pull(grad_normed)
        grad_attn = grad_resid_one.astype(jnp.bfloat16)
        grad_attn_bias = jnp.sum(grad_attn.astype(jnp.float32), axis=(0, 1))
        grad_attn_weight = jnp.einsum(
            "ble,bld->ed", context_local, grad_attn, preferred_element_type=jnp.float32
        )
        grad_context = jnp.einsum(
            "bld,ed->ble", grad_attn, attn_weight, preferred_element_type=jnp.float32
        ).astype(jnp.bfloat16)
        grad_context_all = lax.all_to_all(
            grad_context, "seq", split_axis=2, concat_axis=1, tiled=True
        )
        grad_heads = split_heads(grad_context_all, HD)
        grad_queries, grad_keys, grad_values = attend_backward(
            queries, keys_heads, values_heads, doc_items, grad_heads, lse_all, score_scale
        )
        grad_query_local, grad_key_local, grad_value_local = (
            lax.all_to_all(
                shortened(join_heads(grad_queries, seq_count)),
                "seq",
                split_axis=1,
                concat_axis=2,
                tiled=True,
            ),
            lax.all_to_all(
                shortened(join_heads(grad_keys, seq_count)),
                "seq",
                split_axis=1,
                concat_axis=2,
                tiled=True,
            ),
            lax.all_to_all(
                shortened(join_heads(grad_values, seq_count)),
                "seq",
                split_axis=1,
                concat_axis=2,
                tiled=True,
            ),
        )
        grad_proj = jnp.concatenate([grad_query_local, grad_key_local, grad_value_local], axis=2)
        grad_query_bias = jnp.sum(grad_query_local.astype(jnp.float32), axis=(0, 1))
        grad_value_bias = jnp.sum(grad_value_local.astype(jnp.float32), axis=(0, 1))
        grad_proj_weight = jnp.einsum(
            "bld,ble->de", inputs, grad_proj, preferred_element_type=jnp.float32
        )
        grad_inputs = grad_resid_one + jnp.einsum(
            "ble,de->bld", grad_proj, proj_weight, preferred_element_type=jnp.float32
        )
        grads_in.append(grad_inputs.astype(jnp.bfloat16))
        terms = (
            grad_proj_weight,
            grad_query_bias,
            grad_value_bias,
            grad_attn_weight,
            grad_attn_bias,
            grad_gain_one,
            grad_shift_one,
            grad_upper_weight,
            grad_upper_bias,
            grad_lower_weight,
            grad_lower_bias,
            grad_gain_two,
            grad_shift_two,
        )
        if micro_index == 0:
            accum = terms
        else:
            accum = tuple((left + right for left, right in zip(accum, terms)))
    accum = lax.psum_scatter(accum, "shard", scatter_dimension=0, tiled=True)
    totals = lax.psum(accum, "seq")
    return (jnp.stack(outputs), jnp.stack(grads_in)) + tuple(totals)


def solution(mesh):
    return jax.shard_map(
        local,
        mesh=mesh,
        in_specs=(
            P(None, "shard", "seq", None),
            P(None, "shard", "seq", None),
            P(None, "shard", "seq"),
            P("shard", None),
            P("shard"),
            P("shard"),
            P("shard", None),
            P("shard"),
            P("shard"),
            P("shard"),
            P("shard", None),
            P("shard"),
            P("shard", None),
            P("shard"),
            P("shard"),
            P("shard"),
        ),
        out_specs=(
            P(None, "shard", "seq", None),
            P(None, "shard", "seq", None),
            P("shard", None),
            P("shard"),
            P("shard"),
            P("shard", None),
            P("shard"),
            P("shard"),
            P("shard"),
            P("shard", None),
            P("shard"),
            P("shard", None),
            P("shard"),
            P("shard"),
            P("shard"),
        ),
        check_vma=False,
    )
```

profile of v0, /device:TPU:0, one launch (start us, length us, event | category | flops | bytes accessed | tf_op | source)
XLA Modules:
  0.0 1814.5 jit_solution(9351495482328978773)
XLA Ops:
  19.6 63.9 %all-reduce.21 = (bf16[768]{0:T(1024)(128)(2,1)S(1)}, bf16[768]{0:T(1024)(128)(2,1)S(1)}, bf16[768]{0:T(1024)(128)(2,1)S(1)}, bf16[768]{0:T(1024)(128)(2,1)S(1)}...) all-reduce(bf16[768]{0:T(1024)(128)(2,1)S(1)} %dynamic-update-slice, ...), channel_id=1, replica_groups=mesh['seq'=2,'shard'=16] {'shard'}, use_global_device_ids=true, to_apply=%add.1 | all-reduce | flops 9216 | bytes 36864
  83.5 6.5 add_convert_fusion.3
  101.1 12.0 all-to-all-done
  116.8 4.9 copy.138
  121.7 9.2 all-to-all-done.1
  130.9 4.6 all-to-all-start.2
  135.6 6.3 add_convert_fusion.2
  144.2 4.9 copy.146
  152.9 4.9 copy.148
  157.8 8.3 all-to-all-done.4
  166.1 4.6 all-to-all-start.5
  171.3 12.0 all_gather.28
  185.2 4.9 copy.150
  214.9 4.8 all-to-all-start.6
  221.1 95.1 %while.52 = (s32[]{:T(128)}, bf16[12,1024,64]{1,2,0:T(8,128)(2,1)}, f32[12,1024,1]{1,2,0:T(1,128)S(1)}, s32[12,1024]{1,0:T(8,128)S(1)}, bf16[12,1024,64]{2,1,0:T...) while((s32[]{:T(128)}, bf16[12,1024,64]{1,2,0:T(8,128)(2,1)}, ...), condition=%wide.region_5.6_spmd, body=%wide.region_0.5_spmd.sunk | while | flops 278134784 | bytes 14360197 | solution.py:81
  316.2 5.2 copy.143
  339.6 5.0 all-to-all-start.3
  358.1 95.1 %while.53 = (s32[]{:T(128)}, bf16[12,1024,64]{1,2,0:T(8,128)(2,1)}, f32[12,1024,1]{1,2,0:T(1,128)S(1)}, s32[12,1024]{1,0:T(8,128)S(1)}, bf16[12,1024,64]{2,1,0:T...) while((s32[]{:T(128)}, bf16[12,1024,64]{1,2,0:T(8,128)(2,1)}, ...), condition=%wide.region_15.16_spmd, body=%wide.region_10.15_spmd.sunk | while | flops 278134784 | bytes 14360197 | solution.py:81
  453.2 5.2 copy.155
  458.4 4.6 all-to-all-start.7
  470.3 5.1 all-to-all-done.7
  481.9 11.1 fusion.137
  493.1 23.7 %fusion.161 = (u8[512,3072]{1,0:T(8,128)(4,1)}, u8[512,3072]{1,0:T(8,128)(4,1)}, u8[512,3072]{1,0:T(8,128)(4,1)}, u8[512,3072]{1,0:T(8,128)(4,1)}, f32[2,512,3072]{2,1,0:T(8,128)}) fusion(f32[3072]{0:T(1024)S(1)} %convert_element_type.224, f32[2,512,3072]{2,1,0:T(8,128)} %fusion.137, bf16[768,3072]{1,0:T(8,128)(2,1)} %all-gather.9.cloned.1.call-done, ...), kind=kOutput, calls=%fused_computation.299 | convolution fusion | flops 4917559296 | bytes 39348224 | tf_op jit(solution)/shard_map/bld,df->blf/dot_general | solution.py:249
  516.8 63.4 %multiply_convert_fusion.5 = (bf16[2,512,3072]{2,1,0:T(8,128)(2,1)}, f32[2,512,3072]{2,1,0:T(8,128)}, bf16[2,512,3072]{2,1,0:T(8,128)(2,1)}, f32[2,512,3072]{2,1,0:T(8,128)}) fusion(f32[2,512,3072]{2,1,0:T(8,128)} %get-tuple-element.568, f32[3072]{0:T(1024)S(1)} %convert_element_type.224, u8[512,3072]{1,0:T(8,128)(4,1)} %get-tuple-element.372, ...), kind=kLoop, calls=%fused_computation.210 | loop fusion | flops 443547648 | bytes 69218304 | tf_op jit(solution)/shard_map/convert_element_type | solution.py:252
  580.2 9.2 fusion.223
  589.5 5.5 fusion.222
  597.0 4.3 fusion.157
  601.3 5.5 convert_reduce_fusion.4
  606.8 19.1 %convert_reduce_fusion = (f32[3072]{0:T(1024)}, bf16[2,512,3072]{2,1,0:T(8,128)(2,1)}) fusion(f32[2,512,3072]{2,1,0:T(8,128)} %get-tuple-element.552, bf16[2,512,768]{2,1,0:T(8,128)(2,1)} %get-tuple-element.495, bf16[3072,768]{1,0:T(8,128)(2,1)} %all-gather.11.cloned.1.call-done, f32[2,512,3072]{2,1,0:T(8,128)} %fusion.137, f32[3072]{0:T(1024)S(1)} %convert_element_type.224), kind=kOutput, calls=%fused_computation.193 | convolution fusion | flops 4885312512 | bytes 37773312 | tf_op jit(solution)/shard_map/bld,fd->blf/dot_general | solution.py:337
  625.9 10.4 add_add_fusion.8
  636.4 18.8 %convert_reduce_fusion.1 = (f32[3072]{0:T(1024)}, bf16[2,512,3072]{2,1,0:T(8,128)(2,1)}) fusion(f32[2,512,3072]{2,1,0:T(8,128)} %get-tuple-element.507, bf16[2,512,768]{2,1,0:T(8,128)(2,1)} %get-tuple-element.548, bf16[3072,768]{1,0:T(8,128)(2,1)} %all-gather.11.cloned.1.call-done, f32[2,512,3072]{2,1,0:T(8,128)} %get-tuple-element.568, ...), kind=kOutput, calls=%fused_computation.194 | convolution fusion | flops 4885312512 | bytes 37773312 | tf_op jit(solution)/shard_map/bld,fd->blf/dot_general | solution.py:337
  655.2 13.7 multiply_reduce_fusion.5
  679.3 4.9 copy.158
  684.2 4.7 all-to-all-start.8
  695.5 9.4 all-to-all-done.8
  717.1 221.3 %while.54 = (s32[]{:T(128)}, bf16[12,1024,64]{1,2,0:T(8,128)(2,1)S(1)}, bf16[12,1024,64]{1,2,0:T(8,128)(2,1)}, bf16[12,1024,64]{1,2,0:T(8,128)(2,1)}, s32[12,102...) while((s32[]{:T(128)}, ...), condition=%wide.region_27.28_spmd, body=%wide.region_24.27_spmd.sunk | while | flops 682294272 | bytes 35578032 | solution.py:132
  938.3 5.2 copy.170
  956.8 10.6 all-to-all-done.11
  975.2 228.9 %while.55 = (s32[]{:T(128)}, bf16[12,1024,64]{1,2,0:T(8,128)(2,1)}, bf16[12,1024,64]{1,2,0:T(8,128)(2,1)}, bf16[12,1024,64]{1,2,0:T(8,128)(2,1)}, s32[12,1024]{1...) while((s32[]{:T(128)}, bf16[12,1024,64]{1,2,0:T(8,128)(2,1)}, ...), condition=%wide.region_35.36_spmd, body=%wide.region_32.35_spmd.sunk | while | flops 682294272 | bytes 35578540 | solution.py:132
  1204.1 4.9 copy.179
  1209.0 4.6 all-to-all-start.13
  1213.7 5.3 copy.167
  1219.0 8.1 all-to-all-done.13
  1227.1 4.6 all-to-all-start.10
  1231.8 4.9 copy.182
  1236.7 8.3 all-to-all-done.10
  1245.0 4.6 all-to-all-start.14
  1249.7 4.9 copy.185
  1263.3 4.6 all-to-all-start.15
  1274.6 5.9 fusion.181
  1287.2 8.3 fusion.126
  1295.5 8.1 copy.205
  1310.4 7.7 fusion.225
  1318.2 10.8 bitcast_add_fusion
  1330.8 8.2 fusion.200
  1339.1 11.4 bitcast_add_fusion.1
  1358.5 8.6 fusion.184
  1367.1 58.1 %reduce-scatter.13.cloned.1.call-done = f32[48,2304]{1,0:T(8,128)} async-done(((f32[768,2304]{1,0:T(8,128)}), f32[48,2304]{1,0:T(8,128)}) %reduce-scatter.13.cloned.1.call-update) | async-done | bytes 442384
  1427.6 64.7 %reduce-scatter.7.cloned.1.call-done = f32[48,768]{1,0:T(8,128)} async-done(((f32[768,768]{1,0:T(8,128)}), f32[48,768]{1,0:T(8,128)}) %reduce-scatter.7.cloned.1.call-update) | async-done | bytes 147472 | tf_op jit(solution)/shard_map/reduce_scatter | solution.py:420
  1492.3 114.4 %reduce-scatter.11.cloned.1.call-done = f32[192,768]{1,0:T(8,128)} async-done(((f32[3072,768]{1,0:T(8,128)}), f32[192,768]{1,0:T(8,128)}) %reduce-scatter.11.cloned.1.call-update) | async-done | bytes 589840 | tf_op jit(solution)/shard_map/reduce_scatter | solution.py:420
  1606.6 115.0 %reduce-scatter.9.cloned.1.call-done = f32[48,3072]{1,0:T(8,128)} async-done(((f32[768,3072]{1,0:T(8,128)}), f32[48,3072]{1,0:T(8,128)}) %reduce-scatter.9.cloned.1.call-update) | async-done | bytes 589840 | tf_op jit(solution)/shard_map/reduce_scatter | solution.py:420
  1723.9 60.3 %all-reduce.18 = (f32[768]{0:T(1024)S(1)}, f32[768]{0:T(1024)S(1)}, f32[768]{0:T(1024)S(1)}, f32[768]{0:T(1024)S(1)}, f32[768]{0:T(1024)S(1)}, /*index=5*/f32[30...) all-reduce(f32[768]{0:T(1024)S(1)} %add.367, ...), channel_id=3, replica_groups=mesh['seq'=2,'shard'=16] {'shard'}, use_global_device_ids=true, to_apply=%region_40.41.clone | all-reduce | flops 9216 | bytes 73728
  1784.9 5.8 all-reduce.19
  1790.7 8.3 fusion.187
  (1045 shorter events, 847.1 us)
Async XLA Ops:
  7.2 76.3 %all-gather.5.cloned.1.call-start = ((), (), s32[]{:S(2)}) async-start(), calls=%async_computation.20 | async-start | bytes 3760128 | tf_op jit(solution)/shard_map/all_gather | solution.py:177
  7.9 458.1 %all-gather.7.cloned.1.call-start = ((), (), s32[]{:S(2)}) async-start(), calls=%async_computation.21 | async-start | bytes 1253376 | tf_op jit(solution)/shard_map/all_gather | solution.py:180
  8.7 473.3 %all-gather.9.cloned.1.call-start = ((), (), s32[]{:S(2)}) async-start(), calls=%async_computation.22 | async-start | bytes 5013504 | tf_op jit(solution)/shard_map/all_gather | solution.py:184
  94.4 18.7 %all-to-all-start = ((bf16[2,512,768]{1,0,2:T(2,128)(2,1)}), bf16[2,512,768]{1,0,2:T(2,128)(2,1)S(1)}, u32[]{:S(2)}, u32[]{:S(2)}) async-start(bf16[2,512,768]{1,0,2:T(2,128)(2,1)} %copy.134), calls=%async_computation | async-start | bytes 3145728 | tf_op jit(solution)/shard_map/all_to_all | solution.py:215
  113.1 17.8 all-to-all-start.1
  130.9 10.9 copy-start.27
  130.9 18.2 %all-to-all-start.2 = ((bf16[2,512,768]{1,0,2:T(2,128)(2,1)}), bf16[2,512,768]{1,0,2:T(2,128)(2,1)}, u32[]{:S(2)}, u32[]{:S(2)}) async-start(bf16[2,512,768]{1,0,2:T(2,128)(2,1)} %copy.138), calls=%async_computation.2 | async-start | bytes 3145728 | tf_op jit(solution)/shard_map/all_to_all | solution.py:225
  149.1 17.0 all-to-all-start.4
  152.9 18.4 %copy-start.79 = (s32[2,2,512]{2,1,0:T(2,128)S(1)}, s32[2,2,512]{2,1,0:T(2,128)}, u32[]{:S(2)}) copy-start(s32[2,2,512]{2,1,0:T(2,128)} %param.26) | copy-start | bytes 24580
  166.1 24.0 %copy-start.26 = (bf16[2,512,768]{1,0,2:T(2,128)(2,1)}, bf16[2,512,768]{1,0,2:T(2,128)(2,1)S(1)}, u32[]{:S(2)}) copy-start(bf16[2,512,768]{1,0,2:T(2,128)(2,1)S(1)} %all-to-all-done.4) | copy-start | bytes 4718596
  166.1 48.7 %all-to-all-start.5 = ((bf16[2,512,768]{1,0,2:T(2,128)(2,1)}), bf16[2,512,768]{1,0,2:T(2,128)(2,1)}, u32[]{:S(2)}, u32[]{:S(2)}) async-start(bf16[2,512,768]{1,0,2:T(2,128)(2,1)} %copy.148), calls=%async_computation.5 | async-start | bytes 3145728 | tf_op jit(solution)/shard_map/all_to_all | solution.py:218
  170.7 409.4 %all-gather.11.cloned.1.call-start = ((), (), s32[]{:S(2)}) async-start(), calls=%async_computation.23 | async-start | bytes 5013504 | tf_op jit(solution)/shard_map/all_gather | solution.py:186
  183.4 485.5 %copy-start.42 = (f32[768]{0:T(1024)}, f32[768]{0:T(1024)S(1)}, u32[]{:S(2)}) copy-start(f32[768]{0:T(1024)S(1)} %convert_element_type.221) | copy-start | bytes 9220
  183.4 406.0 %copy-start.44 = (f32[768]{0:T(1024)}, f32[768]{0:T(1024)S(1)}, u32[]{:S(2)}) copy-start(f32[768]{0:T(1024)S(1)} %convert_element_type.222) | copy-start | bytes 9220
  214.9 124.7 %all-to-all-start.6 = ((bf16[2,512,768]{1,0,2:T(2,128)(2,1)}), bf16[2,512,768]{1,0,2:T(2,128)(2,1)}, u32[]{:S(2)}, u32[]{:S(2)}) async-start(bf16[2,512,768]{1,0,2:T(2,128)(2,1)} %copy.150), calls=%async_computation.6 | async-start | bytes 3145728 | tf_op jit(solution)/shard_map/all_to_all | solution.py:225
  316.2 9.4 copy-start.12
  316.2 9.4 copy-start.50
  316.2 9.4 copy-start.58
  339.6 118.8 %all-to-all-start.3 = ((bf16[2,1024,384]{2,0,1:T(2,128)(2,1)}), bf16[2,1024,384]{2,0,1:T(2,128)(2,1)}, u32[]{:S(2)}, u32[]{:S(2)}) async-start(bf16[2,1024,384]{2,0,1:T(2,128)(2,1)} %copy.143), calls=%async_computation.3 | async-start | bytes 3145728 | tf_op jit(solution)/shard_map/all_to_all | solution.py:238
  453.2 5.2 copy-start.57
  458.4 16.9 all-to-all-start.7
  469.8 23.3 %copy-start.3 = (f32[2,512,768]{2,1,0:T(8,128)}, f32[2,512,768]{2,1,0:T(8,128)S(1)}, u32[]{:S(2)}) copy-start(f32[2,512,768]{2,1,0:T(8,128)S(1)} %get-tuple-element.565) | copy-start | bytes 9437188
  469.8 199.2 %copy-start.55 = (f32[2,512]{1,0:T(2,128)}, f32[2,512]{1,0:T(2,128)S(1)}, u32[]{:S(2)}) copy-start(f32[2,512]{1,0:T(2,128)S(1)} %broadcast_multiply_fusion.3) | copy-start | bytes 12292
  470.3 7.1 copy-start.62
  470.3 198.7 %copy-start.60 = (f32[2,512]{1,0:T(2,128)}, f32[2,512]{1,0:T(2,128)S(1)}, u32[]{:S(2)}) copy-start(f32[2,512]{1,0:T(2,128)S(1)} %fusion.203) | copy-start | bytes 12292
  479.7 189.3 %copy-start.51 = (f32[2,512]{1,0:T(2,128)}, f32[2,512]{1,0:T(2,128)S(1)}, u32[]{:S(2)}) copy-start(f32[2,512]{1,0:T(2,128)S(1)} %broadcast_multiply_fusion.1) | copy-start | bytes 12292
  481.9 11.2 copy-start.64
  481.9 187.1 %copy-start.53 = (f32[2,512]{1,0:T(2,128)}, f32[2,512]{1,0:T(2,128)S(1)}, u32[]{:S(2)}) copy-start(f32[2,512]{1,0:T(2,128)S(1)} %fusion.205) | copy-start | bytes 12292
  516.8 63.4 %copy-start.8 = (f32[2,512,768]{2,1,0:T(8,128)S(1)}, f32[2,512,768]{2,1,0:T(8,128)}, u32[]{:S(2)}) copy-start(f32[2,512,768]{2,1,0:T(8,128)} %copy-done.7) | copy-start | bytes 9437188
  516.8 63.4 %copy-start.84 = (f32[768]{0:T(1024)S(1)}, f32[768]{0:T(1024)}, u32[]{:S(2)}) copy-start(f32[768]{0:T(1024)} %convert_element_type.226) | copy-start | bytes 9220
  580.2 9.2 copy-start.4
  580.2 9.2 copy-start.23
  580.2 9.2 copy-start.85
  589.4 11.9 copy-start.2
  589.5 5.5 copy-start
  589.5 5.5 copy-start.59
  655.2 13.7 copy-start.65
  655.2 13.7 copy-start.63
  655.2 13.8 copy-start.5
  655.2 13.8 copy-start.9
  672.9 16.0 copy-start.20
  684.2 20.7 %all-to-all-start.8 = ((bf16[2,512,768]{1,0,2:T(2,128)(2,1)}), bf16[2,512,768]{1,0,2:T(2,128)(2,1)}, u32[]{:S(2)}, u32[]{:S(2)}) async-start(bf16[2,512,768]{1,0,2:T(2,128)(2,1)} %copy.158), calls=%async_computation.8 | async-start | bytes 3145728 | tf_op jit(solution)/shard_map/all_to_all | solution.py:361
  704.9 238.6 %all-to-all-start.12 = ((bf16[2,512,768]{1,0,2:T(2,128)(2,1)}), bf16[2,512,768]{1,0,2:T(2,128)(2,1)S(1)}, u32[]{:S(2)}, u32[]{:S(2)}) async-start(bf16[2,512,768]{1,0,2:T(2,128)(2,1)} %copy.173), calls=%async_computation.12 | async-start | bytes 3145728 | tf_op jit(solution)/shard_map/all_to_all | solution.py:361
  943.5 24.0 %all-to-all-start.11 = ((bf16[2,1024,384]{2,0,1:T(2,128)(2,1)}), bf16[2,1024,384]{2,0,1:T(2,128)(2,1)S(1)}, u32[]{:S(2)}, u32[]{:S(2)}) async-start(bf16[2,1024,384]{2,0,1:T(2,128)(2,1)} %copy.170), calls=%async_computation.11 | async-start | bytes 3145728 | tf_op jit(solution)/shard_map/all_to_all | solution.py:383
  967.5 241.6 %all-to-all-start.9 = ((bf16[2,1024,384]{2,0,1:T(2,128)(2,1)}), bf16[2,1024,384]{2,0,1:T(2,128)(2,1)S(1)}, u32[]{:S(2)}, u32[]{:S(2)}) async-start(bf16[2,1024,384]{2,0,1:T(2,128)(2,1)} %copy.164), calls=%async_computation.9 | async-start | bytes 3145728 | tf_op jit(solution)/shard_map/all_to_all | solution.py:369
  1209.0 18.1 all-to-all-start.13
  1227.1 17.9 all-to-all-start.10
  1245.0 18.3 %all-to-all-start.14 = ((bf16[2,1024,384]{2,0,1:T(2,128)(2,1)}), bf16[2,1024,384]{2,0,1:T(2,128)(2,1)}, u32[]{:S(2)}, u32[]{:S(2)}) async-start(bf16[2,1024,384]{2,0,1:T(2,128)(2,1)} %copy.182), calls=%async_computation.14 | async-start | bytes 3145728 | tf_op jit(solution)/shard_map/all_to_all | solution.py:376
  1263.3 17.3 all-to-all-start.15
  1267.9 157.2 %reduce-scatter.13.cloned.1.call-start = ((), (), s32[]{:S(2)}) async-start(), calls=%async_computation.27 | async-start | bytes 7520256
  1280.6 5.7 copy-start.92
  1303.6 188.6 %reduce-scatter.7.cloned.1.call-start = ((), (), s32[]{:S(2)}) async-start(), calls=%async_computation.24 | async-start | bytes 2506752 | tf_op jit(solution)/shard_map/reduce_scatter | solution.py:420
  1310.3 7.8 copy-start.32
  1310.3 296.3 %reduce-scatter.11.cloned.1.call-start = ((), (), s32[]{:S(2)}) async-start(), calls=%async_computation.26 | async-start | bytes 10027008 | tf_op jit(solution)/shard_map/reduce_scatter | solution.py:420
  1329.0 10.1 copy-start.52
  1329.0 10.1 copy-start.54
  1329.0 392.6 %reduce-scatter.9.cloned.1.call-start = ((), (), s32[]{:S(2)}) async-start(), calls=%async_computation.25 | async-start | bytes 10027008 | tf_op jit(solution)/shard_map/reduce_scatter | solution.py:420
  1330.8 8.2 copy-start.10
  1350.6 450.4 %all-reduce.24.cloned.1.call-start = ((), (), s32[]{:S(2)}) async-start(), calls=%async_computation.28 | async-start | bytes 5013504 | tf_op jit(solution)/shard_map/psum | solution.py:421
  1367.1 356.3 %copy-start.14 = (bf16[2,1024,384]{2,1,0:T(8,128)(2,1)S(1)}, bf16[2,1024,384]{2,1,0:T(8,128)(2,1)}, u32[]{:S(2)}) copy-start(bf16[2,1024,384]{2,1,0:T(8,128)(2,1)} %copy-done.13) | copy-start | bytes 4718596
  1427.6 296.1 %copy-start.16 = (bf16[2,1024,384]{2,1,0:T(8,128)(2,1)S(1)}, bf16[2,1024,384]{2,1,0:T(8,128)(2,1)}, u32[]{:S(2)}) copy-start(bf16[2,1024,384]{2,1,0:T(8,128)(2,1)} %copy-done.15) | copy-start | bytes 4718596
  1721.6 69.1 %copy-start.73 = (f32[2,512]{1,0:T(2,128)S(1)}, f32[2,512]{1,0:T(2,128)}, u32[]{:S(2)}) copy-start(f32[2,512]{1,0:T(2,128)} %copy-done.72) | copy-start | bytes 12292
  1790.7 8.3 copy-start.41
  1801.0 5.9 copy-start.46
  (54 other events, 138.2 us)
Sparse Core Ops, SparseCore 0:
  10.3 50.1 all-gather.4
  62.8 36.8 all-gather.6
  101.9 51.9 all-gather.8
  173.5 71.0 all-gather.10
  1303.8 121.3 reduce-scatter.12
  1429.4 62.8 reduce-scatter.6
  1496.4 110.2 reduce-scatter.10
  1610.7 110.8 reduce-scatter.8
  1724.1 71.7 all-reduce.23
where the time goes:
time: 1840 us; the launch traced here: 1810 us
  matrix products  727 us (40%)
  waiting for transfers between devices  426 us (23%)
  local copies, waits for them, and re-layouts  277 us (15%)
  other arithmetic  152 us (8%)
  blocking collectives  142 us (8%)
  starting transfers between devices  69.6 us (4%)
  between operations  18.5 us (1%)
    reduce_scatter x3, waiting for transfers between devices, local(): accum = lax.psum_scatter(accum, 'shard', scatter_dimension=0, tiled=True)  294 us
    dot_general x96, matrix products, masked_scores(): jnp.einsum('qe,ke->qk', query_rows, key_head, preferred_element_type=jnp....  160 us
    unnamed x2, blocking collectives  124 us
    dot_general x48, matrix products, one_head(): jnp.dot(soft_probs, value_head, preferred_element_type=jnp.float32)  76.2 us
    dot_general x48, matrix products, one_head(): jnp.einsum('qk,qe->ke', grad_scores, query_rows, preferred_element_type=j...  75.9 us
    dot_general x48, matrix products, one_head(): jnp.einsum('qk,qe->ke', soft_probs.astype(jnp.bfloat16), grad_rows, prefe...  70.9 us
    dot_general x48, matrix products, one_head(): jnp.einsum('qe,ke->qk', grad_rows, value_head, preferred_element_type=jnp...  69.9 us
    dot_general x48, matrix products, one_head(): jnp.dot(grad_scores, key_head, preferred_element_type=jnp.float32)  67.3 us
  transfers between devices with their start and end apart: 25, of which 12 were waited for; matrix products, arithmetic and copies ran while one was open for 56% of the time, Pallas kernels for 0%

commit v1 on v0

v1 whole, which is shorter than its diff:
```python
import jax
import jax.numpy as jnp
from jax import lax
from jax.experimental import pallas as pl
from jax.experimental.pallas import tpu as pltpu
from jax.sharding import PartitionSpec as P

HD = 64
PAIR = 2 * HD
QB = 256
UNIT = 128
eps_norm = 1e-05
masked_score = -1e30
bf16 = jnp.bfloat16
f32 = jnp.float32
NT = (((1,), (1,)), ((), ()))
TN = (((0,), (0,)), ((), ()))


def dot(a, b, dims=(((1,), (0,)), ((), ()))):
    return lax.dot_general(a, b, dims, preferred_element_type=f32)


def window_sizes(seq_length):
    units = seq_length // UNIT
    sizes = [n for n in (2, 3, 4, 5, 6) if n < units]
    return sizes + [units]


def key_windows(doc):
    count, seq_length = doc.shape
    first_doc = doc[:, ::QB]
    last_doc = doc[:, QB - 1 :: QB]
    low = jnp.sum((doc[:, None, :] < first_doc[:, :, None]).astype(jnp.int32), axis=2)
    high = jnp.sum((doc[:, None, :] <= last_doc[:, :, None]).astype(jnp.int32), axis=2)
    low_unit = low // UNIT
    need = (high + UNIT - 1) // UNIT - low_unit
    sizes = window_sizes(seq_length)
    size = jnp.full_like(need, sizes[-1])
    for n in sizes[::-1]:
        size = jnp.where(need <= n, n, size)
    start = jnp.minimum(low_unit, seq_length // UNIT - size)
    return start, size


def head_masks():
    lane = lax.broadcasted_iota(jnp.int32, (1, PAIR), 1)
    first = (lane < HD).astype(f32)
    return first.astype(bf16), (1.0 - first).astype(bf16)


def fwd_body(start_ref, size_ref, q_ref, k_ref, v_ref, dcol_ref, drow_ref, o_ref, lse_ref):
    item = pl.program_id(0)
    seq_length = q_ref.shape[0]
    masks = head_masks()
    first_lane = lax.broadcasted_iota(jnp.int32, (QB, PAIR), 1) < HD

    def step(i, carry):
        rows = pl.ds(pl.multiple_of(i * QB, QB), QB)
        for n in window_sizes(seq_length):

            @pl.when(size_ref[item, i] == n)
            def _():
                keys = pl.ds(pl.multiple_of(start_ref[item, i] * UNIT, UNIT), n * UNIT)
                q = q_ref[rows, :] * jnp.asarray(HD**-0.5, bf16)
                k = k_ref[keys, :]
                v = v_ref[keys, :]
                same = dcol_ref[rows, :] == drow_ref[:, keys]
                outs = []
                lses = []
                for h in range(2):
                    s = jnp.where(same, dot(q * masks[h], k, NT), masked_score)
                    top = jnp.max(s, axis=1, keepdims=True)
                    p = jnp.exp(s - top)
                    total = jnp.sum(p, axis=1, keepdims=True)
                    outs.append(dot(p.astype(bf16), v) * (1.0 / total))
                    lses.append(top + jnp.log(total))
                o_ref[rows, :] = jnp.where(first_lane, outs[0], outs[1]).astype(bf16)
                lse = jnp.where(first_lane, lses[0], lses[1]).T
                lse_ref[0:1, rows] = lse[0:1, :]
                lse_ref[1:2, rows] = lse[HD : HD + 1, :]

        return carry

    lax.fori_loop(0, seq_length // QB, step, 0)


def attend_forward(proj, start, size, doc_col, doc_row):
    count, seq_length, columns = proj.shape
    width = columns // 3
    pairs = width // PAIR

    def part(offset):
        return pl.BlockSpec((None, seq_length, PAIR), lambda s, p, *_: (s, 0, p + offset * pairs))

    return pl.pallas_call(
        fwd_body,
        grid_spec=pltpu.PrefetchScalarGridSpec(
            num_scalar_prefetch=2,
            grid=(count, pairs),
            in_specs=[
                part(0),
                part(1),
                part(2),
                pl.BlockSpec((None, seq_length, 1), lambda s, p, *_: (s, 0, 0)),
                pl.BlockSpec((None, 1, seq_length), lambda s, p, *_: (s, 0, 0)),
            ],
            out_specs=[
                part(0),
                pl.BlockSpec((None, None, 2, seq_length), lambda s, p, *_: (s, p, 0, 0)),
            ],
        ),
        out_shape=[
            jax.ShapeDtypeStruct((count, seq_length, width), bf16),
            jax.ShapeDtypeStruct((count, pairs, 2, seq_length), f32),
        ],
        name="attend_forward",
    )(start, size, proj, proj, proj, doc_col, doc_row)


def bwd_body(
    start_ref, size_ref, q_ref, k_ref, v_ref, dcol_ref, drow_ref, o_ref, do_ref, lse_ref,
    dq_ref, dk_ref, dv_ref, dk_acc, dv_acc,
):
    item = pl.program_id(0)
    seq_length = q_ref.shape[0]
    masks = head_masks()
    first_lane = lax.broadcasted_iota(jnp.int32, (QB, PAIR), 1) < HD
    dk_acc[...] = jnp.zeros_like(dk_acc)
    dv_acc[...] = jnp.zeros_like(dv_acc)

    def step(i, carry):
        rows = pl.ds(pl.multiple_of(i * QB, QB), QB)
        for n in window_sizes(seq_length):

            @pl.when(size_ref[item, i] == n)
            def _():
                keys = pl.ds(pl.multiple_of(start_ref[item, i] * UNIT, UNIT), n * UNIT)
                q = q_ref[rows, :] * jnp.asarray(HD**-0.5, bf16)
                k = k_ref[keys, :]
                v = v_ref[keys, :]
                do = do_ref[rows, :]
                same = dcol_ref[keys, :] == drow_ref[:, rows]
                products = (do.astype(f32) * o_ref[rows, :].astype(f32)).T
                dqs = []
                dk = dv = None
                for h in range(2):
                    qh = q * masks[h]
                    doh = do * masks[h]
                    inner = jnp.sum(products[h * HD : (h + 1) * HD, :], axis=0, keepdims=True)
                    s = dot(k, qh, NT) - lse_ref[h : h + 1, rows]
                    p = jnp.exp(jnp.where(same, s, masked_score))
                    ds = (p * (dot(v, doh, NT) - inner)).astype(bf16)
                    dv_part = dot(p.astype(bf16), doh)
                    dk_part = dot(ds, qh)
                    dv = dv_part if dv is None else dv + dv_part
                    dk = dk_part if dk is None else dk + dk_part
                    dqs.append(dot(ds, k, TN))
                dk_acc[keys, :] += dk
                dv_acc[keys, :] += dv
                dq = jnp.where(first_lane, dqs[0], dqs[1]) * (HD**-0.5)
                dq_ref[rows, :] = dq.astype(bf16)

        return carry

    lax.fori_loop(0, seq_length // QB, step, 0)
    dk_ref[...] = dk_acc[...].astype(bf16)
    dv_ref[...] = dv_acc[...].astype(bf16)


def attend_backward(proj, start, size, doc_col, doc_row, context, d_context, lse):
    count, seq_length, columns = proj.shape
    width = columns // 3
    pairs = width // PAIR

    def part(offset):
        return pl.BlockSpec((None, seq_length, PAIR), lambda s, p, *_: (s, 0, p + offset * pairs))

    grad = jax.ShapeDtypeStruct((count, seq_length, width), bf16)
    return pl.pallas_call(
        bwd_body,
        grid_spec=pltpu.PrefetchScalarGridSpec(
            num_scalar_prefetch=2,
            grid=(count, pairs),
            in_specs=[
                part(0),
                part(1),
                part(2),
                pl.BlockSpec((None, seq_length, 1), lambda s, p, *_: (s, 0, 0)),
                pl.BlockSpec((None, 1, seq_length), lambda s, p, *_: (s, 0, 0)),
                part(0),
                part(0),
                pl.BlockSpec((None, None, 2, seq_length), lambda s, p, *_: (s, p, 0, 0)),
            ],
            out_specs=[part(0), part(0), part(0)],
            scratch_shapes=[
                pltpu.VMEM((seq_length, PAIR), f32),
                pltpu.VMEM((seq_length, PAIR), f32),
            ],
        ),
        out_shape=[grad, grad, grad],
        name="attend_backward",
    )(start, size, proj, proj, proj, doc_col, doc_row, context, d_context, lse)


def norm_parts(resid):
    center = jnp.mean(resid, axis=1, keepdims=True)
    deviate = resid - center
    spread = jnp.mean(deviate * deviate, axis=1, keepdims=True)
    rstd = lax.rsqrt(spread + eps_norm)
    return deviate * rstd, rstd


def norm_back(grad, xhat, rstd):
    return rstd * (
        grad
        - jnp.mean(grad, axis=1, keepdims=True)
        - xhat * jnp.mean(grad * xhat, axis=1, keepdims=True)
    )


def middle_body(
    x_ref, o_ref, g_ref, w_out_ref, w_up_ref, w_down_ref, vec_ref, bias_up_ref,
    out_ref, d_attn_ref, d_context_ref, h1_ref, act_ref, d_up_ref, d_down_ref,
    sums_ref, sums_up_ref, slope_ref,
):
    @pl.when(pl.program_id(0) == 0)
    def _():
        sums_ref[...] = jnp.zeros_like(sums_ref)
        sums_up_ref[...] = jnp.zeros_like(sums_up_ref)

    hidden_units = w_up_ref.shape[1]
    chunk = w_up_ref.shape[0]
    chunks = [slice(c, c + chunk) for c in range(0, hidden_units, chunk)]
    bias_out, gain1, shift1, bias_down, gain2, shift2 = (vec_ref[r : r + 1, :] for r in range(6))
    xhat1, rstd1 = norm_parts(x_ref[...].astype(f32) + dot(o_ref[...], w_out_ref[...]) + bias_out)
    h1 = xhat1 * gain1 + shift1
    h1_low = h1.astype(bf16)
    h1_ref[...] = h1_low
    resid2 = h1 + bias_down
    for c in chunks:
        up = dot(h1_low, w_up_ref[:, c]) + bias_up_ref[:, c]
        cdf = 0.5 + 0.5 * lax.erf(up * (0.5**0.5))
        act = (up * cdf).astype(bf16)
        slope_ref[:, c] = cdf + up * jnp.exp(-0.5 * up * up) * 0.3989422804014327
        act_ref[:, c] = act
        resid2 = resid2 + dot(act, w_down_ref[c, :])
    xhat2, rstd2 = norm_parts(resid2)
    out_ref[...] = (xhat2 * gain2 + shift2).astype(bf16)
    g = g_ref[...].astype(f32)
    d_resid2 = norm_back(g * gain2, xhat2, rstd2)
    d_down = d_resid2.astype(bf16)
    d_down_ref[...] = d_down
    d_h1 = d_resid2
    for c in chunks:
        d_up = (dot(d_down, w_down_ref[c, :], NT) * slope_ref[:, c]).astype(bf16)
        d_up_ref[:, c] = d_up
        sums_up_ref[:, c] += jnp.sum(d_up.astype(f32), axis=0, keepdims=True)
        d_h1 = d_h1 + dot(d_up, w_up_ref[:, c], NT)
    d_attn = norm_back(d_h1 * gain1, xhat1, rstd1).astype(bf16)
    d_attn_ref[...] = d_attn
    d_context_ref[...] = dot(d_attn, w_out_ref[...], NT).astype(bf16)
    rows = (d_attn.astype(f32), d_h1 * xhat1, d_h1, d_down.astype(f32), g * xhat2, g)
    for r, value in enumerate(rows):
        sums_ref[r : r + 1, :] += jnp.sum(value, axis=0, keepdims=True)


def middle(x, context, g, w_out, w_up, w_down, vectors, bias_up):
    tokens, width = x.shape
    hidden_units = w_up.shape[1]
    tile = QB

    def rows(columns):
        return pl.BlockSpec((tile, columns), lambda i: (i, 0))

    def whole(shape, mode=None):
        return pl.BlockSpec(shape, lambda i: (0, 0), pipeline_mode=mode)

    once = pl.Buffered(1)
    narrow = jax.ShapeDtypeStruct((tokens, width), bf16)
    wide = jax.ShapeDtypeStruct((tokens, hidden_units), bf16)
    return pl.pallas_call(
        middle_body,
        grid=(tokens // tile,),
        in_specs=[
            rows(width),
            rows(width),
            rows(width),
            whole(w_out.shape, once),
            whole(w_up.shape, once),
            whole(w_down.shape, once),
            whole(vectors.shape, once),
            whole(bias_up.shape, once),
        ],
        out_specs=[
            rows(width),
            rows(width),
            rows(width),
            rows(width),
            rows(hidden_units),
            rows(hidden_units),
            rows(width),
            whole((8, width)),
            whole((1, hidden_units)),
        ],
        out_shape=[
            narrow,
            narrow,
            narrow,
            narrow,
            wide,
            wide,
            narrow,
            jax.ShapeDtypeStruct((8, width), f32),
            jax.ShapeDtypeStruct((1, hidden_units), f32),
        ],
        scratch_shapes=[pltpu.VMEM((tile, hidden_units), f32)],
        name="middle",
    )(x, context, g, w_out, w_up, w_down, vectors, bias_up)


def gather_rows(part):
    return lax.all_gather(part, "shard", axis=0, tiled=True)


def own_sum(part):
    return lax.psum(lax.psum_scatter(part, "shard", scatter_dimension=0, tiled=True), "seq")


def own_sum_low(part):
    piece = lax.psum_scatter(part.astype(bf16), "shard", scatter_dimension=0, tiled=True)
    return jnp.sum(lax.all_gather(piece, "seq").astype(f32), axis=0)


def local(
    hidden, cotangent, segments, w_qkv, bias_q, bias_v, w_out, bias_out, norm1_gain, norm1_bias,
    w_up, bias_up, w_down, bias_down, norm2_gain, norm2_bias,
):
    micro, batch, part_length, width = hidden.shape

    def to_whole(rows):
        merged = rows.reshape((micro * batch,) + rows.shape[2:])
        return lax.all_to_all(merged, "seq", split_axis=0, concat_axis=1, tiled=True)

    def to_parts(rows):
        back = lax.all_to_all(rows, "seq", split_axis=1, concat_axis=0, tiled=True)
        return back.reshape(hidden.shape)

    x = to_whole(hidden)
    doc = to_whole(segments)
    count, seq_length = doc.shape
    tokens = count * seq_length
    start, size = key_windows(doc)
    doc_col = doc[:, :, None]
    doc_row = doc[:, None, :]
    full_qkv = gather_rows(w_qkv)
    narrow = jnp.stack(
        [bias_q, bias_v, bias_out, norm1_gain, norm1_bias, bias_down, norm2_gain, norm2_bias]
    )
    small = jnp.concatenate([narrow.reshape(-1), bias_up])[None, :]
    small = gather_rows(small).astype(f32)
    split = narrow.size
    vectors = small[:, :split].reshape(-1, 8, narrow.shape[1]).transpose(1, 0, 2).reshape(8, width)
    full_bias_up = small[:, split:].reshape(1, -1)
    full_out = gather_rows(w_out)
    full_up = gather_rows(w_up)
    full_down = gather_rows(w_down)
    g = to_whole(cotangent)

    x_rows = x.reshape(tokens, width)
    offsets = jnp.concatenate([vectors[0], jnp.zeros_like(vectors[0]), vectors[1]])
    proj = (dot(x_rows, full_qkv) + offsets).astype(bf16).reshape(count, seq_length, -1)
    context, lse = attend_forward(proj, start, size, doc_col, doc_row)
    context_rows = context.reshape(tokens, width)
    out, d_attn, d_context, h1, act, d_up, d_down, sums, sums_up = middle(
        x_rows,
        context_rows,
        g.reshape(tokens, width),
        full_out,
        full_up,
        full_down,
        vectors[2:],
        full_bias_up,
    )
    layer_out = to_parts(out.reshape(count, seq_length, width))
    grad_down = own_sum_low(dot(act, d_down, TN))
    grad_up = own_sum_low(dot(h1, d_up, TN))
    grad_out = own_sum_low(dot(context_rows, d_attn, TN))
    dq, dk, dv = attend_backward(
        proj,
        start,
        size,
        doc_col,
        doc_row,
        context,
        d_context.reshape(count, seq_length, width),
        lse,
    )
    d_proj = [d.reshape(tokens, width) for d in (dq, dk, dv)]
    grad_qkv = own_sum_low(jnp.concatenate([dot(x_rows, d, TN) for d in d_proj], axis=1))
    grad_x = d_attn.astype(f32)
    for index, d in enumerate(d_proj):
        grad_x = grad_x + dot(d, full_qkv[:, index * width : (index + 1) * width], NT)
    grad_hidden = to_parts(grad_x.astype(bf16).reshape(count, seq_length, width))
    sum_q, sum_v = (jnp.sum(d_proj[i].astype(f32), axis=0) for i in (0, 2))
    shards = width // narrow.shape[1]
    stacked = jnp.concatenate([sum_q[None], sum_v[None], sums[:6]], axis=0)
    stacked = stacked.reshape(8, shards, -1).transpose(1, 0, 2).reshape(shards, -1)
    stacked = jnp.concatenate([stacked, sums_up.reshape(shards, -1)], axis=1)
    totals = own_sum(stacked)[0]
    owned = totals[:split].reshape(8, -1)
    return (
        layer_out,
        grad_hidden,
        grad_qkv,
        owned[0],
        owned[1],
        grad_out,
        owned[2],
        owned[3],
        owned[4],
        grad_up,
        totals[split:],
        grad_down,
        owned[5],
        owned[6],
        owned[7],
    )


def solution(mesh):
    tokens = P(None, "shard", "seq", None)
    matrix = P("shard", None)
    vector = P("shard")
    params = (
        matrix, vector, vector, matrix, vector, vector, vector, matrix, vector, matrix, vector,
        vector, vector,
    )
    return jax.shard_map(
        local,
        mesh=mesh,
        in_specs=(tokens, tokens, P(None, "shard", "seq")) + params,
        out_specs=(tokens, tokens) + params,
        check_vma=False,
    )
```

time: 1840 us -> 665 us (0.36)
  matrix products: 727 us -> 74.1 us
  waiting for transfers between devices: 426 us -> 110 us
  local copies, waits for them, and re-layouts: 277 us -> 43.1 us
  Pallas kernels: 0 us -> 172 us
  other arithmetic: 152 us -> 9.11 us
  blocking collectives: 142 us -> 215 us
  starting transfers between devices: 69.6 us -> 17.3 us
    dot_general x360 -> x10, matrix products: 727 us -> 74.1 us  [dot(): return lax.dot_general(a, b, dims, preferred_element_type=f32)]
    reduce_scatter x3 -> x4, waiting for transfers between devices: 294 us -> 72.4 us  [own_sum_low(): lax.psum_scatter(part.astype(bf16), 'shard', scatter_dimension=0, tiled=T...]
    pallas_call x0 -> x3, Pallas kernels: none -> 172 us  [the longest x1 68.2 us: middle(): pl.pallas_call(middle_body, grid=(tokens // tile,), in_specs=[rows(width)...]
    convert_element_type x57 -> x0, other arithmetic: 77.3 us -> none  [the longest x1 63.4 us: local(): activated = gelu_exact(upper_pre).astype(jnp.bfloat16)]
    slice x80 -> x8, local copies, waits for them, and re-layouts: 67.8 us -> 1.47 us  [the longest x2 0.7 us: local(): vectors[2:]]
    unnamed x10 -> x8, waiting for transfers between devices: 60.7 us -> 2.65 us
    all_to_all x16 -> x3, starting transfers between devices: 69 us -> 16.6 us  [the longest x2 12.5 us: to_parts(): back = lax.all_to_all(rows, 'seq', split_axis=1, concat_axis=0, tiled=True)]
    all_to_all x0 -> x2, blocking collectives: none -> 50.2 us  [to_whole(): lax.all_to_all(merged, 'seq', split_axis=0, concat_axis=1, tiled=True)]
  transfers between devices with their start and end apart: 25 -> 11, of which waited for: 12 -> 4; matrix products, arithmetic and copies ran while one was open for 56% -> 16% of each run, Pallas kernels for 0% -> 7%
where the time goes in v1:
time: 665 us; the launch traced here: 656 us
  blocking collectives  215 us (32%)
  Pallas kernels  172 us (26%)
  waiting for transfers between devices  110 us (17%)
  matrix products  74.1 us (11%)
  local copies, waits for them, and re-layouts  43.1 us (6%)
  starting transfers between devices  17.3 us (3%)
  between operations  15.7 us (2%)
  other arithmetic  9.11 us (1%)
    unnamed x2, blocking collectives  131 us
    dot_general x10, matrix products, dot(): return lax.dot_general(a, b, dims, preferred_element_type=f32)  74.1 us
    reduce_scatter x4, waiting for transfers between devices, own_sum_low(): lax.psum_scatter(part.astype(bf16), 'shard', scatter_dimension=0, tiled=T...  72.4 us
    pallas_call x1, Pallas kernels, middle(): pl.pallas_call(middle_body, grid=(tokens // tile,), in_specs=[rows(width)...  68.2 us
    pallas_call x1, Pallas kernels, attend_backward(): pl.pallas_call(bwd_body, grid_spec=pltpu.PrefetchScalarGridSpec(num_scala...  57.3 us
    all_to_all x2, blocking collectives, to_whole(): lax.all_to_all(merged, 'seq', split_axis=0, concat_axis=1, tiled=True)  50.2 us
    pallas_call x1, Pallas kernels, attend_forward(): pl.pallas_call(fwd_body, grid_spec=pltpu.PrefetchScalarGridSpec(num_scala...  46.3 us
    all_gather x4, blocking collectives, own_sum_low(): return jnp.sum(lax.all_gather(piece, 'seq').astype(f32), axis=0)  28.6 us
  transfers between devices with their start and end apart: 11, of which 4 were waited for; matrix products, arithmetic and copies ran while one was open for 16% of the time, Pallas kernels for 7%

profile of v1, /device:TPU:0, one launch (start us, length us, event | category | flops | bytes accessed | tf_op | source)
XLA Modules:
  0.0 656.5 jit_solution(16885609240223214265)
XLA Ops:
  7.2 0.7 all-gather.10.cloned.1.call-update
  8.0 0.7 all-gather.12.cloned.1.call-update
  8.7 0.7 all-gather.14.cloned.1.call-update
  9.4 0.5 all-gather.16.cloned.1.call-update
  10.0 8.1 %all_to_all.73 = s32[2,2,512]{2,1,0:T(2,128)S(1)} all-to-all(s32[2,2,512]{2,1,0:T(2,128)} %param.18), channel_id=1, replica_groups=mesh['seq'=2,'shard'=16] {'seq'}, dimensions={0} | all-to-all | bytes 16384 | tf_op jit(solution)/shard_map/all_to_all | solution.py:343
  18.0 42.1 %all_to_all.74 = bf16[4,512,768]{2,1,0:T(8,128)(2,1)} all-to-all(bf16[4,512,768]{2,1,0:T(8,128)(2,1)} %bitcast.113), channel_id=1, replica_groups=mesh['seq'=2,'shard'=16] {'seq'}, dimensions={0} | all-to-all | bytes 6291456 | tf_op jit(solution)/shard_map/all_to_all | solution.py:343
  60.2 4.1 all-to-all-start.2
  64.6 0.6 fusion.9
  66.1 59.9 %all-reduce = bf16[9216]{0:T(1024)(128)(2,1)S(1)} all-reduce(bf16[9216]{0:T(1024)(128)(2,1)S(1)} %dynamic-update-slice), channel_id=2, replica_groups=mesh['seq'=2,'shard'=16] {'shard'}, use_global_device_ids=true, to_apply=%add | all-reduce | flops 9216 | bytes 36864
  126.4 0.7 slice.92.vec_ref
  127.1 0.7 reshape.138.bias_up_ref
  128.0 1.4 copy.62.dcol_ref
  129.3 0.6 broadcast_in_dim.29.drow_ref
  130.2 0.6 subtract_minimum_fusion
  130.8 3.8 copy.59
  134.5 1.8 copy.63
  136.3 12.3 %add_convert_fusion = bf16[2048,2304]{1,0:T(8,128)(2,1)} fusion(bf16[2048,768]{1,0:T(8,128)(2,1)} %bitcast.106, bf16[768,2304]{1,0:T(8,128)(2,1)} %all-gather.10.cloned.1.call-done, f32[2304]{0:T(1024)S(1)} %pad_maximum_fusion.2), kind=kOutput, calls=%fused_computation | convolution fusion | flops 7257194496 | bytes 16131072 | tf_op jit(solution)/shard_map/dot_general | solution.py:21
  148.7 46.3 %attend_forward.1 = (bf16[2,1024,768]{2,1,0:T(8,128)(2,1)}, f32[2,6,2,1024]{3,2,1,0:T(2,128)}) custom-call(s32[2,4]{1,0:T(2,128)} %get-tuple-element.90.start_ref, s32[2,4]{1,0:T(2,128)} %get-tuple-element.91.size_ref, bf16[2,1024,2304]{2,1,0:T(8,128)(2,1)} %bitcast.94, bf16[2,1024,2304]{2,1,0:T(8,128)(2,1)} %bitcast.95, bf16[2,1024,2304]{2,1,0:T(8,128)(2,1)} %bitcast.96, ...), custom_call_target="tpu_custom_call" | custom-call | tf_op jit(solution)/shard_map/attend_forward/pallas_call | solution.py:96
  195.0 12.6 %all-gather.16.cloned.1.call-done.w_down_ref = bf16[3072,768]{1,0:T(8,128)(2,1)} async-done(((bf16[192,768]{1,0:T(8,128)(2,1)}), bf16[3072,768]{1,0:T(8,128)(2,1)}) %all-gather.16.cloned.1.call-update) | async-done | bytes 4718608 | tf_op jit(solution)/shard_map/all_gather | solution.py:323
  207.6 68.2 %middle.1 = (bf16[2048,768]{1,0:T(8,128)(2,1)}, bf16[2048,768]{1,0:T(8,128)(2,1)}, bf16[2048,768]{1,0:T(8,128)(2,1)}, bf16[2048,768]{1,0:T(8,128)(2,1)}, bf16[20...) custom-call(bf16[2048,768]{1,0:T(8,128)(2,1)} %bitcast.107, ...), custom_call_target="tpu_custom_call" | custom-call | tf_op jit(solution)/shard_map/middle/pallas_call | solution.py:282
  275.9 57.3 %attend_backward.1 = (bf16[2,1024,768]{2,1,0:T(8,128)(2,1)}, bf16[2,1024,768]{2,1,0:T(8,128)(2,1)}, bf16[2,1024,768]{2,1,0:T(8,128)(2,1)}) custom-call(s32[2,4]{1,0:T(2,128)} %get-tuple-element.90.start_ref, s32[2,4]{1,0:T(2,128)} %get-tuple-element.91.size_ref, bf16[2,1024,2304]{2,1,0:T(8,128)(2,1)} %bitcast.97, bf16[2,1024,2304]{2,1,0:T(8,128)(2,1)} %bitcast.98, ...), custom_call_target="tpu_custom_call" | custom-call | tf_op jit(solution)/shard_map/attend_backward/pallas_call | solution.py:180
  333.2 5.7 fusion
  338.9 3.8 convolution_convert_fusion.2
  343.0 4.7 fusion.1
  347.8 2.7 fusion.2
  350.5 0.4 pad_maximum_fusion
  350.9 4.1 copy.73
  355.0 1.8 copy-done.23
  356.8 14.6 %convolution_convert_fusion = bf16[3072,768]{1,0:T(8,128)(2,1)} fusion(bf16[2048,3072]{1,0:T(8,128)(2,1)} %get-tuple-element.41, bf16[2048,768]{1,0:T(8,128)(2,1)S(1)} %copy-done.23), kind=kOutput, calls=%fused_computation.4 | convolution fusion | flops 9666035712 | bytes 20447232 | tf_op jit(solution)/shard_map/dot_general | solution.py:21
  371.5 0.3 reduce-scatter.9.cloned.1.call-start
  371.7 1.6 copy-done.21
  373.4 14.5 %convolution_convert_fusion.1 = bf16[768,3072]{1,0:T(8,128)(2,1)} fusion(bf16[2048,768]{1,0:T(8,128)(2,1)S(1)} %copy-done.21, bf16[2048,3072]{1,0:T(8,128)(2,1)} %get-tuple-element.40), kind=kOutput, calls=%fused_computation.5 | convolution fusion | flops 9666035712 | bytes 20447232 | tf_op jit(solution)/shard_map/dot_general | solution.py:21
  387.8 1.9 copy-done.2
  389.7 6.0 fusion.6
  395.7 4.7 fusion.4
  400.4 2.3 copy-done.24
  402.6 5.2 add_convert_fusion.1
  407.8 4.9 copy.67
  412.7 7.3 %all-to-all-start.4 = ((bf16[2,1024,768]{2,0,1:T(2,128)(2,1)}), bf16[2,1024,768]{2,0,1:T(2,128)(2,1)S(1)}, u32[]{:S(2)}, u32[]{:S(2)}) async-start(bf16[2,1024,768]{2,0,1:T(2,128)(2,1)} %copy.67), calls=%async_computation.4 | async-start | bytes 6291456 | tf_op jit(solution)/shard_map/all_to_all | solution.py:346
  420.0 6.8 %copy.64 = bf16[2,1024,768]{2,0,1:T(2,128)(2,1)} copy(bf16[2,1024,768]{2,1,0:T(8,128)(2,1)} %bitcast.119) | data formatting | bytes 6291456 | tf_op jit(solution)/shard_map/reshape | solution.py:385
  426.8 22.8 %all-to-all-done.4 = bf16[2,1024,768]{2,0,1:T(2,128)(2,1)S(1)} async-done(((bf16[2,1024,768]{2,0,1:T(2,128)(2,1)}), bf16[2,1024,768]{2,0,1:T(2,128)(2,1)S(1)}, u32[]{:S(2)}, u32[]{:S(2)}) %all-to-all-start.4) | async-done | bytes 3145760 | tf_op jit(solution)/shard_map/all_to_all | solution.py:346
  449.6 5.2 all-to-all-start.3
  454.8 3.9 convert_reduce_fusion
  459.1 0.5 broadcast.63
  459.6 0.7 reduce.5
  460.4 71.2 %all-reduce.1 = f32[16,576]{1,0:T(8,128)S(1)} all-reduce(f32[16,576]{1,0:T(8,128)S(1)} %pad_maximum_fusion.1), channel_id=8, replica_groups=mesh['seq'=2,'shard'=16] {'shard'}, use_global_device_ids=true, to_apply=%region_6.7.clone | all-reduce | flops 9216 | bytes 73728
  531.6 0.7 constant_dynamic-slice_fusion
  532.3 4.9 psum.7
  537.2 0.6 slice.121
  537.8 0.6 slice_bitcast_fusion
  538.4 0.4 copy.68
  538.8 1.9 copy.72
  540.7 2.3 copy.65
  543.0 1.9 copy.71
  544.9 6.0 all-gather.2
  550.8 0.7 convert_reduce_fusion.5
  551.5 6.8 %all-gather.1 = bf16[96,2304]{1,0:T(8,128)(2,1)S(1)} all-gather(bf16[48,2304]{1,0:T(8,128)(2,1)} %reduce-scatter.13.cloned.1.call-done), channel_id=3, replica_groups=mesh['seq'=2,'shard'=16] {'seq'}, dimensions={0}, use_global_device_ids=true | all-gather | bytes 663552 | tf_op jit(solution)/shard_map/all_gather | solution.py:332
  558.3 0.8 convert_reduce_fusion.4
  559.1 2.4 reduce-scatter.11.cloned.1.call-done
  561.5 7.8 %all-gather.4 = bf16[384,768]{1,0:T(8,128)(2,1)S(1)} all-gather(bf16[192,768]{1,0:T(8,128)(2,1)} %reduce-scatter.11.cloned.1.call-done), channel_id=6, replica_groups=mesh['seq'=2,'shard'=16] {'seq'}, dimensions={0}, use_global_device_ids=true | all-gather | bytes 884736 | tf_op jit(solution)/shard_map/all_gather | solution.py:332
  569.3 0.9 convert_reduce_fusion.2
  570.2 70.0 %reduce-scatter.9.cloned.1.call-done = bf16[48,3072]{1,0:T(8,128)(2,1)} async-done(((bf16[768,3072]{1,0:T(8,128)(2,1)}), bf16[48,3072]{1,0:T(8,128)(2,1)}) %reduce-scatter.9.cloned.1.call-update) | async-done | bytes 294928 | tf_op jit(solution)/shard_map/reduce_scatter | solution.py:331
  640.2 8.1 %all-gather.3 = bf16[96,3072]{1,0:T(8,128)(2,1)S(1)} all-gather(bf16[48,3072]{1,0:T(8,128)(2,1)} %reduce-scatter.9.cloned.1.call-done), channel_id=5, replica_groups=mesh['seq'=2,'shard'=16] {'seq'}, dimensions={0}, use_global_device_ids=true | all-gather | bytes 884736 | tf_op jit(solution)/shard_map/all_gather | solution.py:332
  648.3 0.9 convert_reduce_fusion.3
  (92 shorter events, 2.2 us)
Async XLA Ops:
  7.2 129.2 %all-gather.10.cloned.1.call-start = ((), (), s32[]{:S(2)}) async-start(), calls=%async_computation.9 | async-start | bytes 3760128 | tf_op jit(solution)/shard_map/all_gather | solution.py:323
  7.9 187.1 %all-gather.12.cloned.1.call-start = ((), (), s32[]{:S(2)}) async-start(), calls=%async_computation.10 | async-start | bytes 1253376 | tf_op jit(solution)/shard_map/all_gather | solution.py:323
  8.7 186.3 %all-gather.14.cloned.1.call-start = ((), (), s32[]{:S(2)}) async-start(), calls=%async_computation.11 | async-start | bytes 5013504 | tf_op jit(solution)/shard_map/all_gather | solution.py:323
  9.4 198.2 %all-gather.16.cloned.1.call-start = ((), (), s32[]{:S(2)}) async-start(), calls=%async_computation.12 | async-start | bytes 5013504 | tf_op jit(solution)/shard_map/all_gather | solution.py:323
  60.2 4.2 copy-start.9
  60.2 4.3 copy-start.10
  60.2 4.3 copy-start.11
  60.2 4.3 copy-start.12
  60.2 4.3 copy-start.13
  60.2 4.3 copy-start.14
  60.2 4.3 copy-start.15
  60.2 4.3 copy-start.16
  60.2 4.4 copy-start.8
  60.2 5.6 copy-start.17
  60.2 74.3 %all-to-all-start.2 = ((bf16[4,512,768]{2,1,0:T(8,128)(2,1)}), bf16[4,512,768]{2,1,0:T(8,128)(2,1)S(1)}, u32[]{:S(2)}, u32[]{:S(2)}) async-start(bf16[4,512,768]{2,1,0:T(8,128)(2,1)} %bitcast.114), calls=%async_computation.2 | async-start | bytes 6291456 | tf_op jit(solution)/shard_map/all_to_all | solution.py:343
  64.3 480.5 %reduce-scatter.7.cloned.1.call-start = ((), (), s32[]{:S(2)}) async-start(), calls=%async_computation.13 | async-start | bytes 1253376 | tf_op jit(solution)/shard_map/reduce_scatter | solution.py:331
  275.9 57.3 %copy-start.1 = (bf16[2,2,512,768]{3,2,1,0:T(8,128)(2,1)S(1)}, bf16[2,2,512,768]{3,2,1,0:T(8,128)(2,1)}, u32[]{:S(2)}) copy-start(bf16[2,2,512,768]{3,2,1,0:T(8,128)(2,1)} %copy.59) | copy-start | bytes 9437188
  333.2 5.7 copy-start
  333.2 5.7 copy-start.19
  342.8 208.7 %reduce-scatter.13.cloned.1.call-start = ((), (), s32[]{:S(2)}) async-start(), calls=%async_computation.16 | async-start | bytes 3760128 | tf_op jit(solution)/shard_map/reduce_scatter | solution.py:331
  343.0 4.7 copy-start.3
  347.7 2.7 copy-start.5
  355.0 1.9 copy-start.23
  355.0 206.5 %reduce-scatter.11.cloned.1.call-start = ((), (), s32[]{:S(2)}) async-start(), calls=%async_computation.15 | async-start | bytes 5013504 | tf_op jit(solution)/shard_map/reduce_scatter | solution.py:331
  371.4 1.9 copy-start.21
  371.5 268.8 %reduce-scatter.9.cloned.1.call-start = ((), (), s32[]{:S(2)}) async-start(), calls=%async_computation.14 | async-start | bytes 5013504 | tf_op jit(solution)/shard_map/reduce_scatter | solution.py:331
  387.8 1.9 copy-start.2
  389.7 6.0 copy-start.18
  389.7 6.0 copy-start.22
  395.7 4.7 copy-start.4
  395.7 4.7 copy-start.20
  395.7 6.9 %copy-start.24 = (f32[2048,768]{1,0:T(8,128)S(1)}, f32[2048,768]{1,0:T(8,128)}, u32[]{:S(2)}) copy-start(f32[2048,768]{1,0:T(8,128)} %fusion.6) | copy-start | bytes 18874372
  412.7 36.9 %all-to-all-start.4 = ((bf16[2,1024,768]{2,0,1:T(2,128)(2,1)}), bf16[2,1024,768]{2,0,1:T(2,128)(2,1)S(1)}, u32[]{:S(2)}, u32[]{:S(2)}) async-start(bf16[2,1024,768]{2,0,1:T(2,128)(2,1)} %copy.67), calls=%async_computation.4 | async-start | bytes 6291456 | tf_op jit(solution)/shard_map/all_to_all | solution.py:346
  449.6 91.1 %all-to-all-start.3 = ((bf16[2,1024,768]{2,0,1:T(2,128)(2,1)}), bf16[2,1024,768]{2,0,1:T(2,128)(2,1)}, u32[]{:S(2)}, u32[]{:S(2)}) async-start(bf16[2,1024,768]{2,0,1:T(2,128)(2,1)} %copy.64), calls=%async_computation.3 | async-start | bytes 6291456 | tf_op jit(solution)/shard_map/all_to_all | solution.py:346
  454.8 4.1 copy-start.6
  454.8 4.8 copy-start.7
Sparse Core Ops, SparseCore 0:
  10.3 49.8 all-gather.9
  62.4 36.9 all-gather.11
  101.8 51.9 all-gather.13
  155.9 51.6 all-gather.15
  342.9 69.2 reduce-scatter.6
  415.9 67.0 reduce-scatter.12
  486.9 74.6 reduce-scatter.10
  565.4 74.8 reduce-scatter.8

commit v2 on v1

v2 whole, which is shorter than its diff:
```python
import functools

import jax
import jax.numpy as jnp
from jax import lax
from jax.experimental import pallas as pl
from jax.experimental.pallas import tpu as pltpu
from jax.sharding import PartitionSpec as P


HD = 64
PAIR = 2 * HD
QB = 256
UNIT = 128
GROUPS = 1
eps_norm = 1e-05
masked_score = -1e30
bf16 = jnp.bfloat16
f32 = jnp.float32
NT = (((1,), (1,)), ((), ()))
TN = (((0,), (0,)), ((), ()))


def dot(a, b, dims=(((1,), (0,)), ((), ()))):
    return lax.dot_general(a, b, dims, preferred_element_type=f32)


def window_sizes(seq_length):
    units = seq_length // UNIT
    sizes = [n for n in (2, 3, 4, 5, 6) if n < units]
    return sizes + [units]


def key_windows(doc):
    _, seq_length = doc.shape
    first_doc = doc[:, ::QB]
    last_doc = doc[:, QB - 1 :: QB]
    low = jnp.sum((doc[:, None, :] < first_doc[:, :, None]).astype(jnp.int32), axis=2)
    high = jnp.sum((doc[:, None, :] <= last_doc[:, :, None]).astype(jnp.int32), axis=2)
    low_unit = low // UNIT
    need = (high + UNIT - 1) // UNIT - low_unit
    sizes = window_sizes(seq_length)
    size = jnp.full_like(need, sizes[-1])
    for n in sizes[::-1]:
        size = jnp.where(need <= n, n, size)
    start = jnp.minimum(low_unit, seq_length // UNIT - size)
    return start, size


def head_masks():
    lane = lax.broadcasted_iota(jnp.int32, (1, PAIR), 1)
    first = (lane < HD).astype(f32)
    return first.astype(bf16), (1.0 - first).astype(bf16)


def fwd_body(start_ref, size_ref, q_ref, k_ref, v_ref, dcol_ref, drow_ref, o_ref, lse_ref):
    item = pl.program_id(0)
    seq_length = q_ref.shape[0]
    masks = head_masks()
    first_lane = lax.broadcasted_iota(jnp.int32, (QB, PAIR), 1) < HD

    def step(i, carry):
        rows = pl.ds(pl.multiple_of(i * QB, QB), QB)
        for n in window_sizes(seq_length):

            @pl.when(size_ref[item, i] == n)
            def _():
                keys = pl.ds(pl.multiple_of(start_ref[item, i] * UNIT, UNIT), n * UNIT)
                q = q_ref[rows, :] * jnp.asarray(HD**-0.5, bf16)
                k = k_ref[keys, :]
                v = v_ref[keys, :]
                same = dcol_ref[rows, :] == drow_ref[:, keys]
                outs = []
                lses = []
                for h in range(2):
                    s = jnp.where(same, dot(q * masks[h], k, NT), masked_score)
                    top = jnp.max(s, axis=1, keepdims=True)
                    p = jnp.exp(s - top)
                    total = jnp.sum(p, axis=1, keepdims=True)
                    outs.append(dot(p.astype(bf16), v) * (1.0 / total))
                    lses.append(top + jnp.log(total))
                o_ref[rows, :] = jnp.where(first_lane, outs[0], outs[1]).astype(bf16)
                lse = jnp.where(first_lane, lses[0], lses[1]).T
                lse_ref[0:1, rows] = lse[0:1, :]
                lse_ref[1:2, rows] = lse[HD : HD + 1, :]

        return carry

    lax.fori_loop(0, seq_length // QB, step, 0)


def column_block(seq_length, base):
    return pl.BlockSpec((None, seq_length, PAIR), lambda s, p, *_: (s, 0, p + base))


def attend_forward(proj, start, size, doc_col, doc_row, group):
    count, seq_length, columns = proj.shape
    all_pairs = columns // 3 // PAIR
    pairs = all_pairs // GROUPS

    def part(index):
        return column_block(seq_length, index * all_pairs + group * pairs)

    return pl.pallas_call(
        fwd_body,
        grid_spec=pltpu.PrefetchScalarGridSpec(
            num_scalar_prefetch=2,
            grid=(count, pairs),
            in_specs=[
                part(0),
                part(1),
                part(2),
                pl.BlockSpec((None, seq_length, 1), lambda s, p, *_: (s, 0, 0)),
                pl.BlockSpec((None, 1, seq_length), lambda s, p, *_: (s, 0, 0)),
            ],
            out_specs=[
                column_block(seq_length, 0),
                pl.BlockSpec((None, None, 2, seq_length), lambda s, p, *_: (s, p, 0, 0)),
            ],
        ),
        out_shape=[
            jax.ShapeDtypeStruct((count, seq_length, pairs * PAIR), bf16),
            jax.ShapeDtypeStruct((count, pairs, 2, seq_length), f32),
        ],
        cost_estimate=pl.CostEstimate(
            flops=16 * count * pairs * seq_length**2 * PAIR, transcendentals=0, bytes_accessed=0
        ),
        name="attend_forward",
    )(start, size, proj, proj, proj, doc_col, doc_row)


def bwd_body(
    start_ref, size_ref, q_ref, k_ref, v_ref, dcol_ref, drow_ref, o_ref, do_ref, lse_ref,
    grad_ref, sums_ref, dk_acc, dv_acc,
):
    item = pl.program_id(0)
    seq_length = q_ref.shape[0]
    masks = head_masks()
    first_lane = lax.broadcasted_iota(jnp.int32, (QB, PAIR), 1) < HD
    dk_acc[...] = jnp.zeros_like(dk_acc)
    dv_acc[...] = jnp.zeros_like(dv_acc)
    sums_ref[...] = jnp.zeros_like(sums_ref)

    def step(i, carry):
        rows = pl.ds(pl.multiple_of(i * QB, QB), QB)
        for n in window_sizes(seq_length):

            @pl.when(size_ref[item, i] == n)
            def _():
                keys = pl.ds(pl.multiple_of(start_ref[item, i] * UNIT, UNIT), n * UNIT)
                q = q_ref[rows, :] * jnp.asarray(HD**-0.5, bf16)
                k = k_ref[keys, :]
                v = v_ref[keys, :]
                do = do_ref[rows, :]
                same = dcol_ref[keys, :] == drow_ref[:, rows]
                products = (do.astype(f32) * o_ref[rows, :].astype(f32)).T
                dqs = []
                dk = dv = None
                for h in range(2):
                    qh = q * masks[h]
                    doh = do * masks[h]
                    inner = jnp.sum(products[h * HD : (h + 1) * HD, :], axis=0, keepdims=True)
                    s = dot(k, qh, NT) - lse_ref[h : h + 1, rows]
                    p = jnp.exp(jnp.where(same, s, masked_score))
                    ds = (p * (dot(v, doh, NT) - inner)).astype(bf16)
                    dv_part = dot(p.astype(bf16), doh)
                    dk_part = dot(ds, qh)
                    dv = dv_part if dv is None else dv + dv_part
                    dk = dk_part if dk is None else dk + dk_part
                    dqs.append(dot(ds, k, TN))
                dk_acc[keys, :] += dk
                dv_acc[keys, :] += dv
                dq = (jnp.where(first_lane, dqs[0], dqs[1]) * (HD**-0.5)).astype(bf16)
                grad_ref[0, rows, :] = dq
                sums_ref[0:1, :] += jnp.sum(dq.astype(f32), axis=0, keepdims=True)

        return carry

    lax.fori_loop(0, seq_length // QB, step, 0)
    grad_ref[1] = dk_acc[...].astype(bf16)
    dv = dv_acc[...].astype(bf16)
    grad_ref[2] = dv
    sums_ref[1:2, :] = jnp.sum(dv.astype(f32), axis=0, keepdims=True)


def attend_backward(proj, start, size, doc_col, doc_row, context, d_context, lse, group):
    count, seq_length, columns = proj.shape
    all_pairs = columns // 3 // PAIR
    pairs = all_pairs // GROUPS

    def part(index):
        return column_block(seq_length, index * all_pairs + group * pairs)

    return pl.pallas_call(
        bwd_body,
        grid_spec=pltpu.PrefetchScalarGridSpec(
            num_scalar_prefetch=2,
            grid=(count, pairs),
            in_specs=[
                part(0),
                part(1),
                part(2),
                pl.BlockSpec((None, seq_length, 1), lambda s, p, *_: (s, 0, 0)),
                pl.BlockSpec((None, 1, seq_length), lambda s, p, *_: (s, 0, 0)),
                column_block(seq_length, 0),
                column_block(seq_length, 0),
                pl.BlockSpec((None, None, 2, seq_length), lambda s, p, *_: (s, p, 0, 0)),
            ],
            out_specs=[
                pl.BlockSpec((3, None, seq_length, PAIR), lambda s, p, *_: (0, s, 0, p)),
                pl.BlockSpec((None, 2, PAIR), lambda s, p, *_: (s, 0, p)),
            ],
            scratch_shapes=[
                pltpu.VMEM((seq_length, PAIR), f32),
                pltpu.VMEM((seq_length, PAIR), f32),
            ],
        ),
        out_shape=[
            jax.ShapeDtypeStruct((3, count, seq_length, pairs * PAIR), bf16),
            jax.ShapeDtypeStruct((count, 2, pairs * PAIR), f32),
        ],
        cost_estimate=pl.CostEstimate(
            flops=24 * count * pairs * seq_length**2 * PAIR, transcendentals=0, bytes_accessed=0
        ),
        name="attend_backward",
    )(start, size, proj, proj, proj, doc_col, doc_row, context, d_context, lse)


def norm_parts(resid):
    center = jnp.mean(resid, axis=1, keepdims=True)
    deviate = resid - center
    spread = jnp.mean(deviate * deviate, axis=1, keepdims=True)
    rstd = lax.rsqrt(spread + eps_norm)
    return deviate * rstd, rstd


def norm_back(grad, xhat, rstd):
    return rstd * (
        grad
        - jnp.mean(grad, axis=1, keepdims=True)
        - xhat * jnp.mean(grad * xhat, axis=1, keepdims=True)
    )


def middle_body(
    x_ref, g_ref, w_out_ref, vec_ref, bias_up_ref, *refs
):
    chunk = x_ref.shape[1]
    chunks = [slice(c, c + chunk) for c in range(0, bias_up_ref.shape[1], chunk)]
    w_up_refs, refs = refs[: len(chunks)], refs[len(chunks) :]
    w_down_refs, refs = refs[: len(chunks)], refs[len(chunks) :]
    o_refs, refs = refs[:GROUPS], refs[GROUPS:]
    d_context_refs, refs = refs[:GROUPS], refs[GROUPS:]
    out_ref, d_attn_ref, h1_ref, act_ref, d_up_ref, d_down_ref, sums_ref, sums_up_ref, slope_ref = refs
    span = o_refs[0].shape[1]

    @pl.when(pl.program_id(0) == 0)
    def _():
        sums_ref[...] = jnp.zeros_like(sums_ref)
        sums_up_ref[...] = jnp.zeros_like(sums_up_ref)

    bias_out, gain1, shift1, bias_down, gain2, shift2 = (vec_ref[r : r + 1, :] for r in range(6))
    resid1 = x_ref[...].astype(f32) + bias_out
    for j, o_ref in enumerate(o_refs):
        resid1 = resid1 + dot(o_ref[...], w_out_ref[j * span : (j + 1) * span, :])
    xhat1, rstd1 = norm_parts(resid1)
    h1 = xhat1 * gain1 + shift1
    h1_low = h1.astype(bf16)
    h1_ref[...] = h1_low
    resid2 = h1 + bias_down
    for c, w_up_ref, w_down_ref in zip(chunks, w_up_refs, w_down_refs):
        up = dot(h1_low, w_up_ref[...]) + bias_up_ref[:, c]
        cdf = 0.5 + 0.5 * lax.erf(up * (0.5**0.5))
        act = (up * cdf).astype(bf16)
        slope_ref[:, c] = cdf + up * jnp.exp(-0.5 * up * up) * 0.3989422804014327
        act_ref[:, c] = act
        resid2 = resid2 + dot(act, w_down_ref[...])
    xhat2, rstd2 = norm_parts(resid2)
    out_ref[...] = (xhat2 * gain2 + shift2).astype(bf16)
    g = g_ref[...].astype(f32)
    d_resid2 = norm_back(g * gain2, xhat2, rstd2)
    d_down = d_resid2.astype(bf16)
    d_down_ref[...] = d_down
    d_h1 = d_resid2
    for c, w_up_ref, w_down_ref in zip(chunks, w_up_refs, w_down_refs):
        d_up = (dot(d_down, w_down_ref[...], NT) * slope_ref[:, c]).astype(bf16)
        d_up_ref[:, c] = d_up
        sums_up_ref[:, c] += jnp.sum(d_up.astype(f32), axis=0, keepdims=True)
        d_h1 = d_h1 + dot(d_up, w_up_ref[...], NT)
    d_attn = norm_back(d_h1 * gain1, xhat1, rstd1).astype(bf16)
    d_attn_ref[...] = d_attn
    for j, ref in enumerate(d_context_refs):
        ref[...] = dot(d_attn, w_out_ref[j * span : (j + 1) * span, :], NT).astype(bf16)
    rows = (d_attn.astype(f32), d_h1 * xhat1, d_h1, d_down.astype(f32), g * xhat2, g)
    for r, value in enumerate(rows):
        sums_ref[r : r + 1, :] += jnp.sum(value, axis=0, keepdims=True)


def middle(x, contexts, g, w_packed, vectors, bias_up):
    tokens, width = x.shape
    hidden_units = bias_up.shape[1]
    blocks = hidden_units // width
    tile = QB

    def rows(columns):
        return pl.BlockSpec((tile, columns), lambda i: (i, 0))

    def whole(shape, mode=None):
        return pl.BlockSpec(shape, lambda i: (0, 0), pipeline_mode=mode)

    once = pl.Buffered(1)

    def square(index):
        return pl.BlockSpec((width, width), lambda i: (0, index), pipeline_mode=once)

    narrow = jax.ShapeDtypeStruct((tokens, width), bf16)
    wide = jax.ShapeDtypeStruct((tokens, hidden_units), bf16)
    return pl.pallas_call(
        middle_body,
        grid=(tokens // tile,),
        in_specs=[
            rows(width),
            rows(width),
            square(0),
            whole(vectors.shape, once),
            whole(bias_up.shape, once),
        ]
        + [square(1 + c) for c in range(2 * blocks)]
        + [rows(width // GROUPS)] * GROUPS,
        out_specs=[rows(width // GROUPS)] * GROUPS
        + [
            rows(width),
            rows(width),
            rows(width),
            rows(hidden_units),
            rows(hidden_units),
            rows(width),
            whole((8, width)),
            whole((1, hidden_units)),
        ],
        out_shape=[jax.ShapeDtypeStruct((tokens, width // GROUPS), bf16)] * GROUPS
        + [
            narrow,
            narrow,
            narrow,
            wide,
            wide,
            narrow,
            jax.ShapeDtypeStruct((8, width), f32),
            jax.ShapeDtypeStruct((1, hidden_units), f32),
        ],
        scratch_shapes=[pltpu.VMEM((tile, hidden_units), f32)],
        cost_estimate=pl.CostEstimate(
            flops=6 * tokens * width * (2 * hidden_units + width), transcendentals=0, bytes_accessed=0
        ),
        name="middle",
    )(
        x, g, w_packed, vectors, bias_up, *[w_packed] * (2 * blocks), *contexts
    )


def send(part, axis, size, target):
    return lax.ppermute(part, axis, [(i, target(i)) for i in range(size)])


def blocks_first(array, shards, blocks):
    split = array.reshape(array.shape[0], shards, blocks, -1)
    return split.transpose(0, 2, 1, 3).reshape(array.shape)


def shards_first(array, shards, blocks):
    return blocks_first(array, blocks, shards)


def gather_rows(part):
    return lax.all_gather(part, "shard", axis=0, tiled=True)


def reduce_rows(grad):
    return lax.psum_scatter(grad, "shard", scatter_dimension=0, tiled=True)


def reduce_parts(piece, parts):
    total = piece.astype(f32)
    for shift in range(1, parts):
        total = total + send(piece, "seq", parts, lambda i: (i + shift) % parts).astype(f32)
    return total


def after(value, *earlier):
    return lax.optimization_barrier((value,) + earlier)


def to_whole(rows, parts):
    count = rows.shape[0] * rows.shape[1] // parts
    blocks = rows.reshape((parts, count) + rows.shape[2:])
    index = lax.axis_index("seq")
    whole = jnp.zeros((count, parts) + rows.shape[2:], rows.dtype)
    for shift in range(parts):
        block = lax.dynamic_index_in_dim(blocks, (index + shift) % parts, 0, keepdims=False)
        if shift:
            block = lax.ppermute(block, "seq", [(i, (i + shift) % parts) for i in range(parts)])
        whole = lax.dynamic_update_index_in_dim(whole, block, (index - shift) % parts, 1)
    return whole.reshape((count, parts * rows.shape[2]) + rows.shape[3:])


def to_parts(rows, parts, shape):
    count = rows.shape[0]
    blocks = rows.reshape((count, parts, rows.shape[1] // parts) + rows.shape[2:])
    index = lax.axis_index("seq")
    back = jnp.zeros((parts, count) + blocks.shape[2:], rows.dtype)
    for shift in range(parts):
        block = lax.dynamic_index_in_dim(blocks, (index + shift) % parts, 1, keepdims=False)
        if shift:
            block = lax.ppermute(block, "seq", [(i, (i + shift) % parts) for i in range(parts)])
        back = lax.dynamic_update_index_in_dim(back, block, (index - shift) % parts, 0)
    return back.reshape(shape)


def local(
    shards, parts, hidden, cotangent, segments, w_qkv, bias_q, bias_v, w_out, bias_out, norm1_gain,
    norm1_bias, w_up, bias_up, w_down, bias_down, norm2_gain, norm2_bias,
):
    width = hidden.shape[3]
    owned_rows = w_qkv.shape[0]
    columns = w_qkv.shape[1]
    narrow = jnp.concatenate(
        [bias_q, bias_v, bias_out, norm1_gain, norm1_bias, bias_down, norm2_gain, norm2_bias]
    )
    small = jnp.concatenate([narrow, bias_up]).reshape(owned_rows, -1)
    spare = -small.shape[1] % UNIT
    packed = jnp.concatenate([w_qkv, jnp.pad(small, ((0, 0), (0, spare)))], axis=1)
    doc = to_whole(segments, parts)
    x = to_whole(hidden, parts)
    packed_full = gather_rows(packed)
    full_qkv = packed_full[:, :columns]
    small_full = packed_full[:, columns : columns + small.shape[1]].reshape(shards, -1).astype(f32)
    split = narrow.shape[0]
    vectors = small_full[:, :split].reshape(shards, 8, -1).transpose(1, 0, 2).reshape(8, width)
    full_bias_up = blocks_first(small_full[:, split:].reshape(1, -1), shards, w_down.shape[0] // owned_rows)
    blocks = w_down.shape[0] // owned_rows
    rest = jnp.concatenate(
        [w_out, blocks_first(w_up, shards, blocks)]
        + [w_down[b * owned_rows : (b + 1) * owned_rows] for b in range(blocks)],
        axis=1,
    )
    rest, packed_full = after(rest, packed_full)
    rest_full = gather_rows(rest)
    ahead = width + w_up.shape[1]

    count, seq_length = doc.shape
    tokens = count * seq_length
    start, size = key_windows(doc)
    doc_col = doc[:, :, None]
    doc_row = doc[:, None, :]
    x_rows = x.reshape(tokens, width)
    g = to_whole(cotangent, parts)
    offsets = jnp.concatenate([vectors[0], jnp.zeros_like(vectors[0]), vectors[1]])
    proj = (dot(x_rows, full_qkv) + offsets).astype(bf16).reshape(count, seq_length, -1)
    context, lse = attend_forward(proj, start, size, doc_col, doc_row, 0)
    context_rows = context.reshape(tokens, width)
    results = middle(
        x_rows,
        [context_rows],
        g.reshape(tokens, width),
        rest_full,
        vectors[2:],
        full_bias_up,
    )
    d_context, out, d_attn, h1, act, d_up, d_down, sums, sums_up = results
    grad_rest = jnp.concatenate(
        [
            dot(context_rows, d_attn, TN).astype(bf16),
            dot(h1, d_up, TN).astype(bf16),
        ]
        + [
            dot(act[:, b * width : (b + 1) * width], d_down, TN).astype(bf16)
            for b in range(blocks)
        ],
        axis=1,
    )
    d_context, out, grad_rest = after(d_context, out, grad_rest)
    layer_out = to_parts(out.reshape(count, seq_length, width), parts, hidden.shape)
    grad_rest = reduce_rows(grad_rest)
    d_proj, d_sums = attend_backward(
        proj,
        start,
        size,
        doc_col,
        doc_row,
        context,
        d_context.reshape(count, seq_length, width),
        lse,
        0,
    )
    d_rows = [d_proj[index].reshape(tokens, width) for index in range(3)]
    stacked = jnp.concatenate([jnp.sum(d_sums, axis=0), sums[:6]], axis=0)
    stacked = stacked.reshape(8, shards, -1).transpose(1, 0, 2).reshape(shards, -1)
    sums_up = shards_first(sums_up, shards, blocks)
    stacked = jnp.concatenate([stacked, sums_up.reshape(shards, -1)], axis=1)
    stacked = jnp.pad(stacked.reshape(width, -1), ((0, 0), (0, spare))).astype(bf16)
    grad_packed = jnp.concatenate(
        [dot(x_rows, d, TN).astype(bf16) for d in d_rows] + [stacked], axis=1
    )
    d_attn, grad_packed = after(d_attn, grad_packed)
    grad_packed = reduce_rows(grad_packed)
    grad_x = d_attn.astype(f32)
    for index, d in enumerate(d_rows):
        grad_x = grad_x + dot(d, full_qkv[:, index * width : (index + 1) * width], NT)
    grad_x = grad_x.astype(bf16).reshape(count, seq_length, width)
    grad_hidden = to_parts(grad_x, parts, hidden.shape)
    grad_rest = reduce_parts(grad_rest, parts)
    grad_out = grad_rest[:, :width]
    grad_up = shards_first(grad_rest[:, width:ahead], shards, blocks)
    grad_down = jnp.concatenate(
        [grad_rest[:, ahead + b * width : ahead + (b + 1) * width] for b in range(blocks)]
    )
    grad_packed = reduce_parts(grad_packed, parts)
    totals = grad_packed[:, columns : columns + small.shape[1]].reshape(-1)
    owned = totals[:split].reshape(8, -1)
    return (
        layer_out,
        grad_hidden,
        grad_packed[:, :columns],
        owned[0],
        owned[1],
        grad_out,
        owned[2],
        owned[3],
        owned[4],
        grad_up,
        totals[split:],
        grad_down,
        owned[5],
        owned[6],
        owned[7],
    )


def whole_step(shards, parts, *arguments):
    return local(shards, parts, *arguments)


def solution(mesh):
    tokens = P(None, "shard", "seq", None)
    matrix = P("shard", None)
    vector = P("shard")
    params = (
        matrix, vector, vector, matrix, vector, vector, vector, matrix, vector, matrix, vector,
        vector, vector,
    )
    return jax.shard_map(
        functools.partial(whole_step, mesh.shape["shard"], mesh.shape["seq"]),
        mesh=mesh,
        in_specs=(tokens, tokens, P(None, "shard", "seq")) + params,
        out_specs=(tokens, tokens) + params,
        check_vma=False,
    )
```

time: 665 us -> 653 us (0.982)
  blocking collectives: 215 us -> 0 us
  waiting for transfers between devices: 110 us -> 281 us
  local copies, waits for them, and re-layouts: 43.1 us -> 77.2 us
  Pallas kernels: 172 us -> 184 us
  starting transfers between devices: 17.3 us -> 7.24 us
    unnamed x2 -> x0, blocking collectives: 131 us -> none
    ppermute x0 -> x7, waiting for transfers between devices: none -> 102 us  [the longest x3 60.6 us: to_whole(): lax.ppermute(block, 'seq', [(i, (i + shift) % parts) for i in range(parts)])]
    reduce_scatter x4 -> x2, waiting for transfers between devices: 72.4 us -> 138 us  [reduce_rows(): return lax.psum_scatter(grad, 'shard', scatter_dimension=0, tiled=True)]
    all_to_all x2 -> x0, blocking collectives: 50.2 us -> none  [to_whole(): lax.all_to_all(merged, 'seq', split_axis=0, concat_axis=1, tiled=True)]
    all_gather x4 -> x0, blocking collectives: 28.6 us -> none  [own_sum_low(): return jnp.sum(lax.all_gather(piece, 'seq').astype(f32), axis=0)]
    all_gather x4 -> x2, waiting for transfers between devices: 12.7 us -> 40 us  [gather_rows(): return lax.all_gather(part, 'shard', axis=0, tiled=True)]
    all_to_all x3 -> x0, waiting for transfers between devices: 22.8 us -> none  [the longest x2 22.8 us: to_parts(): back = lax.all_to_all(rows, 'seq', split_axis=1, concat_axis=0, tiled=True)]
    all_to_all x3 -> x0, starting transfers between devices: 16.6 us -> none  [the longest x2 12.5 us: to_parts(): back = lax.all_to_all(rows, 'seq', split_axis=1, concat_axis=0, tiled=True)]
  transfers between devices with their start and end apart: 11 -> 11, of which waited for: 4 -> 8; matrix products, arithmetic and copies ran while one was open for 16% -> 12% of each run, Pallas kernels for 7% -> 8%
where the time goes in v2:
time: 653 us; the launch traced here: 648 us
  waiting for transfers between devices  281 us (43%)
  Pallas kernels  184 us (28%)
  local copies, waits for them, and re-layouts  77.2 us (12%)
  matrix products  72.6 us (11%)
  between operations  14.5 us (2%)
  other arithmetic  11.5 us (2%)
  starting transfers between devices  7.24 us (1%)
    reduce_scatter x2, waiting for transfers between devices, reduce_rows(): return lax.psum_scatter(grad, 'shard', scatter_dimension=0, tiled=True)  138 us
    dot_general x13, matrix products, dot(): return lax.dot_general(a, b, dims, preferred_element_type=f32)  72.6 us
    pallas_call x1, Pallas kernels, middle(): pl.pallas_call(middle_body, grid=(tokens // tile,), in_specs=[rows(width)...  67.2 us
    pallas_call x1, Pallas kernels, attend_backward(): pl.pallas_call(bwd_body, grid_spec=pltpu.PrefetchScalarGridSpec(num_scala...  65.7 us
    ppermute x3, waiting for transfers between devices, to_whole(): lax.ppermute(block, 'seq', [(i, (i + shift) % parts) for i in range(parts)])  60.6 us
    pallas_call x1, Pallas kernels, attend_forward(): pl.pallas_call(fwd_body, grid_spec=pltpu.PrefetchScalarGridSpec(num_scala...  51.3 us
    all_gather x2, waiting for transfers between devices, gather_rows(): return lax.all_gather(part, 'shard', axis=0, tiled=True)  40 us
    ppermute x2, waiting for transfers between devices, to_parts(): lax.ppermute(block, 'seq', [(i, (i + shift) % parts) for i in range(parts)])  34.9 us
  transfers between devices with their start and end apart: 11, of which 8 were waited for; matrix products, arithmetic and copies ran while one was open for 12% of the time, Pallas kernels for 8%

profile of v2, /device:TPU:0, one launch (start us, length us, event | category | flops | bytes accessed | tf_op | source)
XLA Modules:
  0.0 648.2 jit_solution(12015786287427278289)
XLA Ops:
  7.2 6.1 concatenate.30
  13.4 1.6 fusion.42
  15.2 1.7 reshape.116
  17.1 1.4 reshape.117
  19.9 1.5 slice_dynamic-update-slice_fusion.3
  21.4 1.5 slice_dynamic-update-slice_fusion.2
  23.0 1.5 slice_dynamic-update-slice_fusion.1
  24.5 1.5 slice_dynamic-update-slice_fusion
  26.0 40.0 %all-gather.3.cloned.1.call-done = bf16[768,2432]{1,0:T(8,128)(2,1)} async-done(((bf16[48,2432]{1,0:T(8,128)(2,1)}), bf16[768,2432]{1,0:T(8,128)(2,1)}) %all-gather.3.cloned.1.call-update) | async-done | bytes 3735568 | tf_op jit(solution)/shard_map/all_gather | solution.py:376
  66.1 2.7 dynamic-slice_bitcast_fusion.3
  68.8 1.5 collective-permute-start
  70.2 1.2 dynamic-slice_bitcast_fusion.2
  72.0 1.5 collective-permute-start.2
  73.7 1.9 bitcast_dynamic-update-slice_fusion.7
  75.6 1.9 broadcast.53.clone.2
  77.5 1.2 bitcast_dynamic-update-slice_fusion.5
  78.8 60.6 %collective-permute-done.2 = s32[2,512]{1,0:T(2,128)S(1)} collective-permute-done((s32[2,512]{1,0:T(2,128)S(1)}, s32[2,512]{1,0:T(2,128)S(1)}, u32[]{:S(2)}, u32[]{:S(2)}) %collective-permute-start.2) | collective-permute-done | bytes 4128 | tf_op jit(solution)/shard_map/ppermute | solution.py:402
  140.1 1.9 broadcast_in_dim_reshape.10.dcol_ref
  143.5 1.6 bitcast_dynamic-update-slice_fusion.6
  145.1 3.8 bitcast_dynamic-update-slice_fusion.4
  148.9 1.0 slice_convert_fusion
  149.8 0.8 reshape.130
  153.9 11.8 %add_convert_fusion = bf16[2048,2304]{1,0:T(8,128)(2,1)} fusion(bf16[2048,768]{1,0:T(8,128)(2,1)S(1)} %bitcast.81, f32[2304]{0:T(1024)S(1)} %pad_maximum_fusion.2, bf16[768,2432]{1,0:T(8,128)(2,1)} %all-gather.3.cloned.1.call-done), kind=kOutput, calls=%fused_computation | convolution fusion | flops 7257194496 | bytes 16131072 | tf_op jit(solution)/shard_map/dot_general | solution.py:25
  165.7 51.3 %attend_forward.1 = (bf16[2,1024,768]{2,1,0:T(8,128)(2,1)}, f32[2,6,2,1024]{3,2,1,0:T(2,128)}) custom-call(s32[2,4]{1,0:T(2,128)} %get-tuple-element.117.start_ref, s32[2,4]{1,0:T(2,128)} %get-tuple-element.118.size_ref, bf16[2,1024,2304]{2,1,0:T(8,128)(2,1)} %bitcast.99, bf16[2,1024,2304]{2,1,0:T(8,128)(2,1)} %bitcast.100, ...), custom_call_target="tpu_custom_call" | custom-call | flops 25769803776 | tf_op jit(solution)/shard_map/attend_forward/pallas_call | solution.py:104
  217.0 67.2 %middle.1 = (bf16[2048,768]{1,0:T(8,128)(2,1)}, bf16[2048,768]{1,0:T(8,128)(2,1)}, bf16[2048,768]{1,0:T(8,128)(2,1)}, bf16[2048,768]{1,0:T(8,128)(2,1)}, bf16[20...) custom-call(bf16[2048,768]{1,0:T(8,128)(2,1)} %bitcast.82, ...), custom_call_target="tpu_custom_call" | custom-call | flops 65229815808 | tf_op jit(solution)/shard_map/middle/pallas_call | solution.py:318
  284.3 5.5 convolution_convert_fusion.4
  290.4 1.2 constant_dynamic-update-slice_fusion.2
  291.6 16.1 %fusion.1 = bf16[768,6912]{1,0:T(8,128)(2,1)} fusion(bf16[768,6912]{1,0:T(8,128)(2,1)} %constant_dynamic-update-slice_fusion.2, bf16[2048,768]{1,0:T(8,128)(2,1)} %get-tuple-element.39, bf16[2048,3072]{1,0:T(8,128)(2,1)} %get-tuple-element.40), kind=kOutput, calls=%fused_computation.5 | convolution fusion | flops 9666035712 | bytes 20447232 | tf_op jit(solution)/shard_map/dot_general | solution.py:25
  307.7 3.9 fusion.15
  311.6 3.8 fusion.21
  315.4 3.9 fusion.27
  319.3 3.8 fusion.33
  323.1 65.7 %attend_backward.1 = (bf16[3,2,1024,768]{3,2,1,0:T(8,128)(2,1)}, f32[2,2,768]{2,1,0:T(2,128)}) custom-call(s32[2,4]{1,0:T(2,128)} %get-tuple-element.117.start_ref, s32[2,4]{1,0:T(2,128)} %get-tuple-element.118.size_ref, bf16[2,1024,2304]{2,1,0:T(8,128)(2,1)} %bitcast.102, bf16[2,1024,2304]{2,1,0:T(8,128)(2,1)} %bitcast.103, ...), custom_call_target="tpu_custom_call" | custom-call | flops 38654705664 | tf_op jit(solution)/shard_map/attend_backward/pallas_call | solution.py:194
  388.8 4.4 fusion.44
  393.4 3.8 convolution_convert_fusion.2
  397.3 3.8 convolution_convert_fusion.3
  401.1 3.7 convolution_convert_fusion.1
  405.7 3.5 fusion.2
  409.2 6.0 copy.127
  415.9 5.1 fusion.39
  421.0 2.7 fusion.37
  423.7 4.6 add_convert_fusion.1
  428.6 1.7 copy-done.8
  430.2 1.2 dynamic-slice_bitcast_fusion.1
  431.8 1.9 broadcast.53.clone.3
  433.7 1.2 bitcast_dynamic-update-slice_fusion.1
  435.3 30.5 %collective-permute-done.4 = bf16[2,512,768]{2,1,0:T(8,128)(2,1)S(1)} collective-permute-done((bf16[2,512,768]{2,1,0:T(8,128)(2,1)S(1)}, bf16[2,512,768]{2,1,0:T(8,128)(2,1)S(1)}, u32[]{:S(2)}, u32[]{:S(2)}) %collective-permute-start.4) | collective-permute-done | bytes 1572896 | tf_op jit(solution)/shard_map/ppermute | solution.py:415
  465.8 1.2 bitcast_dynamic-update-slice_fusion
  467.1 26.6 %reduce-scatter.7.cloned.1.call-done = bf16[48,2432]{1,0:T(8,128)(2,1)} async-done(((bf16[768,2432]{1,0:T(8,128)(2,1)}), bf16[48,2432]{1,0:T(8,128)(2,1)}) %reduce-scatter.7.cloned.1.call-update) | async-done | bytes 233488 | tf_op jit(solution)/shard_map/reduce_scatter | solution.py:380
  493.7 1.5 collective-permute-start.5
  495.2 4.5 collective-permute-done.3
  499.6 1.6 bitcast_dynamic-update-slice_fusion.2
  501.2 1.3 copy.128
  502.5 0.9 collective-permute-done.5
  503.4 2.1 copy.111
  505.5 111.5 %reduce-scatter.5.cloned.1.call-done = bf16[48,6912]{1,0:T(8,128)(2,1)} async-done(((bf16[768,6912]{1,0:T(8,128)(2,1)}), bf16[48,6912]{1,0:T(8,128)(2,1)}) %reduce-scatter.5.cloned.1.call-update) | async-done | bytes 663568 | tf_op jit(solution)/shard_map/reduce_scatter | solution.py:380
  616.9 1.5 collective-permute-start.6
  618.4 1.5 convert_add_fusion.1
  620.0 1.1 copy.122
  627.5 6.1 collective-permute-done.6
  633.6 1.2 convert_add_fusion
  634.8 0.8 fusion.45
  637.0 2.6 reshape.129
  639.6 1.8 pad_maximum_fusion
  (128 shorter events, 19.1 us)
Async XLA Ops:
  7.2 11.3 %copy-start.11 = (bf16[48,768]{1,0:T(8,128)(2,1)S(1)}, bf16[48,768]{1,0:T(8,128)(2,1)}, u32[]{:S(2)}) copy-start(bf16[48,768]{1,0:T(8,128)(2,1)} %param.22) | copy-start | bytes 221188
  7.2 58.8 %all-gather.3.cloned.1.call-start = ((), (), s32[]{:S(2)}) async-start(), calls=%async_computation.2 | async-start | bytes 3969024 | tf_op jit(solution)/shard_map/all_gather | solution.py:376
  15.1 201.9 %all-gather.5.cloned.1.call-start = ((), (), s32[]{:S(2)}) async-start(), calls=%async_computation.3 | async-start | bytes 11280384 | tf_op jit(solution)/shard_map/all_gather | solution.py:376
  18.5 51.8 %copy-start.6 = (bf16[2,2,512,768]{3,2,1,0:T(8,128)(2,1)S(1)}, bf16[2,2,512,768]{3,2,1,0:T(8,128)(2,1)}, u32[]{:S(2)}) copy-start(bf16[2,2,512,768]{3,2,1,0:T(8,128)(2,1)} %param.17) | copy-start | bytes 9437188
  66.0 427.6 %reduce-scatter.7.cloned.1.call-start = ((), (), s32[]{:S(2)}) async-start(), calls=%async_computation.5 | async-start | bytes 3969024 | tf_op jit(solution)/shard_map/reduce_scatter | solution.py:380
  66.1 5.9 copy-start.15
  68.8 74.7 %collective-permute-start = (bf16[2,512,768]{2,1,0:T(8,128)(2,1)}, bf16[2,512,768]{2,1,0:T(8,128)(2,1)}, u32[]{:S(2)}, u32[]{:S(2)}) collective-permute-start(bf16[2,512,768]{2,1,0:T(8,128)(2,1)} %dynamic-slice_bitcast_fusion.3), channel_id=1, source_target_pairs={{0,16},{16,0},{1,17},{17,1},{2,18},{18,2},{3,19},{19,3},{4,20},{20... | collective-permute-start | bytes 4718600 | tf_op jit(solution)/shard_map/ppermute | solution.py:402
  71.5 73.6 %collective-permute-start.1 = (bf16[2,512,768]{2,1,0:T(8,128)(2,1)}, bf16[2,512,768]{2,1,0:T(8,128)(2,1)}, u32[]{:S(2)}, u32[]{:S(2)}) collective-permute-start(bf16[2,512,768]{2,1,0:T(8,128)(2,1)} %dynamic-slice_bitcast_fusion.2), channel_id=1, source_target_pairs={{0,16},{16,0},{1,17},{17,1},{2,18},{18,2},{3,19},{19,3},{4,20},{20... | collective-permute-start | bytes 4718600 | tf_op jit(solution)/shard_map/ppermute | solution.py:402
  72.0 67.3 %collective-permute-start.2 = (s32[2,512]{1,0:T(2,128)S(1)}, s32[2,512]{1,0:T(2,128)S(1)}, u32[]{:S(2)}, u32[]{:S(2)}) collective-permute-start(s32[2,512]{1,0:T(2,128)S(1)} %get-tuple-element.135), channel_id=1, source_target_pairs={{0,16},{16,0},{1,17},{17,1},{2,18},{18,2},{3,19},{19,3},{4,20},{20... | collective-permute-start | bytes 12296 | tf_op jit(solution)/shard_map/ppermute | solution.py:402
  73.7 3.8 copy-start.7
  145.0 20.7 %copy-start.4 = (bf16[2,2,512,768]{3,2,1,0:T(8,128)(2,1)}, bf16[2,2,512,768]{3,2,1,0:T(8,128)(2,1)S(1)}, u32[]{:S(2)}) copy-start(bf16[2,2,512,768]{3,2,1,0:T(8,128)(2,1)S(1)} %bitcast_dynamic-update-slice_fusion.6) | copy-start | bytes 9437188
  290.4 17.3 %slice-start = ((s8[12582912]{0:T(1024)(128)(4,1)}), s8[4194304]{0:T(1024)(128)(4,1)S(1)}, s32[]{:S(2)}) async-start(s8[12582912]{0:T(1024)(128)(4,1)} %bitcast.108), calls=%async_computation.6 | async-start | bytes 8388608
  291.6 16.1 %slice-start.1 = ((s8[12582912]{0:T(1024)(128)(4,1)}), s8[4194304]{0:T(1024)(128)(4,1)S(1)}, s32[]{:S(2)}) async-start(s8[12582912]{0:T(1024)(128)(4,1)} %bitcast.108), calls=%async_computation.7 | async-start | bytes 8388608
  291.6 16.1 %slice-start.2 = ((s8[12582912]{0:T(1024)(128)(4,1)}), s8[4194304]{0:T(1024)(128)(4,1)S(1)}, s32[]{:S(2)}) async-start(s8[12582912]{0:T(1024)(128)(4,1)} %bitcast.108), calls=%async_computation.8 | async-start | bytes 8388608
  291.6 16.1 %copy-start.17 = (bf16[2048,768]{1,0:T(8,128)(2,1)S(1)}, bf16[2048,768]{1,0:T(8,128)(2,1)}, u32[]{:S(2)}) copy-start(bf16[2048,768]{1,0:T(8,128)(2,1)} %get-tuple-element.42) | copy-start | bytes 9437188
  388.8 4.7 copy-start.5
  393.2 4.1 copy-start
  393.2 4.1 copy-start.2
  401.1 3.7 copy-start.13
  401.1 3.8 copy-start.16
  401.1 4.0 copy-start.12
  415.3 201.7 %reduce-scatter.5.cloned.1.call-start = ((), (), s32[]{:S(2)}) async-start(), calls=%async_computation.4 | async-start | bytes 11280384 | tf_op jit(solution)/shard_map/reduce_scatter | solution.py:380
  415.8 5.1 copy-start.1
  415.9 5.1 copy-start.14
  428.4 1.9 copy-start.8
  428.5 37.3 %collective-permute-start.4 = (bf16[2,512,768]{2,1,0:T(8,128)(2,1)S(1)}, bf16[2,512,768]{2,1,0:T(8,128)(2,1)S(1)}, u32[]{:S(2)}, u32[]{:S(2)}) collective-permute-start(bf16[2,512,768]{2,1,0:T(8,128)(2,1)S(1)} %dynamic-slice_bitcast_fusion), channel_id=1, source_target_pairs={{0,16},{16,0},{1,17},{17,1},{2,18},{18,2},{3,19},{19,3},{4,20},{20... | collective-permute-start | bytes 4718600 | tf_op jit(solution)/shard_map/ppermute | solution.py:415
  431.5 68.1 %collective-permute-start.3 = (bf16[2,512,768]{2,1,0:T(8,128)(2,1)}, bf16[2,512,768]{2,1,0:T(8,128)(2,1)}, u32[]{:S(2)}, u32[]{:S(2)}) collective-permute-start(bf16[2,512,768]{2,1,0:T(8,128)(2,1)} %dynamic-slice_bitcast_fusion.1), channel_id=1, source_target_pairs={{0,16},{16,0},{1,17},{17,1},{2,18},{18,2},{3,19},{19,3},{4,20},{20... | collective-permute-start | bytes 4718600 | tf_op jit(solution)/shard_map/ppermute | solution.py:415
  493.7 7.6 %copy-start.10 = (bf16[48,2432]{1,0:T(8,128)(2,1)S(1)}, bf16[48,2432]{1,0:T(8,128)(2,1)}, u32[]{:S(2)}) copy-start(bf16[48,2432]{1,0:T(8,128)(2,1)} %reduce-scatter.7.cloned.1.call-done) | copy-start | bytes 700420
  493.7 9.7 %collective-permute-start.5 = (bf16[48,2432]{1,0:T(8,128)(2,1)}, bf16[48,2432]{1,0:T(8,128)(2,1)}, u32[]{:S(2)}, u32[]{:S(2)}) collective-permute-start(bf16[48,2432]{1,0:T(8,128)(2,1)} %reduce-scatter.7.cloned.1.call-done), channel_id=1, source_target_pairs={{0,16},{16,0},{1,17},{17,1},{2,18},{18,2},{3,19},{19,3},{4,20},{20... | collective-permute-start | bytes 700424 | tf_op jit(solution)/shard_map/ppermute | solution.py:363
  501.2 115.7 %copy-start.3 = (bf16[2,2,512,768]{3,2,1,0:T(8,128)(2,1)}, bf16[2,2,512,768]{3,2,1,0:T(8,128)(2,1)S(1)}, u32[]{:S(2)}) copy-start(bf16[2,2,512,768]{3,2,1,0:T(8,128)(2,1)S(1)} %bitcast_dynamic-update-slice_fusion.2) | copy-start | bytes 9437188
  616.9 16.6 %collective-permute-start.6 = (bf16[48,6912]{1,0:T(8,128)(2,1)}, bf16[48,6912]{1,0:T(8,128)(2,1)}, u32[]{:S(2)}, u32[]{:S(2)}) collective-permute-start(bf16[48,6912]{1,0:T(8,128)(2,1)} %reduce-scatter.5.cloned.1.call-done), channel_id=1, source_target_pairs={{0,16},{16,0},{1,17},{17,1},{2,18},{18,2},{3,19},{19,3},{4,20},{20... | collective-permute-start | bytes 1990664 | tf_op jit(solution)/shard_map/ppermute | solution.py:363
  618.4 15.1 %copy-start.9 = (bf16[48,6912]{1,0:T(8,128)(2,1)S(1)}, bf16[48,6912]{1,0:T(8,128)(2,1)}, u32[]{:S(2)}) copy-start(bf16[48,6912]{1,0:T(8,128)(2,1)} %reduce-scatter.5.cloned.1.call-done) | copy-start | bytes 1990660
Sparse Core Ops, SparseCore 0:
  15.2 50.7 all-gather.2
  68.3 87.0 all-gather.4
  415.4 78.2 reduce-scatter.6
  497.6 119.3 reduce-scatter.4

commit v3 on v2

--- a/solution.py
+++ b/solution.py
@@ -424,21 +424,22 @@
     width = hidden.shape[3]
     owned_rows = w_qkv.shape[0]
     columns = w_qkv.shape[1]
-    narrow = jnp.concatenate(
-        [bias_q, bias_v, bias_out, norm1_gain, norm1_bias, bias_down, norm2_gain, norm2_bias]
-    )
-    small = jnp.concatenate([narrow, bias_up]).reshape(owned_rows, -1)
+    blocks = w_down.shape[0] // owned_rows
+    narrow = [
+        bias_q, bias_v, bias_out, norm1_gain, norm1_bias, bias_down, norm2_gain, norm2_bias,
+    ]
+    small = jnp.stack(narrow + [row for row in bias_up.reshape(blocks, -1)], axis=1)
     spare = -small.shape[1] % UNIT
     packed = jnp.concatenate([w_qkv, jnp.pad(small, ((0, 0), (0, spare)))], axis=1)
+    x = to_whole(hidden, parts)
     doc = to_whole(segments, parts)
-    x = to_whole(hidden, parts)
+    start, size = key_windows(doc)
+    doc_col = doc[:, :, None]
+    doc_row = doc[:, None, :]
     packed_full = gather_rows(packed)
     full_qkv = packed_full[:, :columns]
-    small_full = packed_full[:, columns : columns + small.shape[1]].reshape(shards, -1).astype(f32)
-    split = narrow.shape[0]
-    vectors = small_full[:, :split].reshape(shards, 8, -1).transpose(1, 0, 2).reshape(8, width)
-    full_bias_up = blocks_first(small_full[:, split:].reshape(1, -1), shards, w_down.shape[0] // owned_rows)
-    blocks = w_down.shape[0] // owned_rows
+    vectors = packed_full[:, columns:].astype(f32).T
+    full_bias_up = vectors[8 : 8 + blocks].reshape(1, -1)
     rest = jnp.concatenate(
         [w_out, blocks_first(w_up, shards, blocks)]
         + [w_down[b * owned_rows : (b + 1) * owned_rows] for b in range(blocks)],
@@ -446,13 +447,9 @@
     )
     rest, packed_full = after(rest, packed_full)
     rest_full = gather_rows(rest)
-    ahead = width + w_up.shape[1]
 
     count, seq_length = doc.shape
     tokens = count * seq_length
-    start, size = key_windows(doc)
-    doc_col = doc[:, :, None]
-    doc_row = doc[:, None, :]
     x_rows = x.reshape(tokens, width)
     g = to_whole(cotangent, parts)
     offsets = jnp.concatenate([vectors[0], jnp.zeros_like(vectors[0]), vectors[1]])
@@ -464,24 +461,24 @@
         [context_rows],
         g.reshape(tokens, width),
         rest_full,
-        vectors[2:],
+        vectors[2:8],
         full_bias_up,
     )
     d_context, out, d_attn, h1, act, d_up, d_down, sums, sums_up = results
-    grad_rest = jnp.concatenate(
-        [
-            dot(context_rows, d_attn, TN).astype(bf16),
-            dot(h1, d_up, TN).astype(bf16),
-        ]
-        + [
-            dot(act[:, b * width : (b + 1) * width], d_down, TN).astype(bf16)
-            for b in range(blocks)
-        ],
+
+    def grad_block(rows, block):
+        return dot(rows[:, block * width : (block + 1) * width], d_down, TN).astype(bf16)
+
+    later = blocks // 2
+    grad_first = jnp.concatenate(
+        [dot(h1, d_up, TN).astype(bf16)] + [grad_block(act, b) for b in range(later, blocks)],
         axis=1,
     )
-    d_context, out, grad_rest = after(d_context, out, grad_rest)
+    d_context, out, act, context_rows, grad_first = after(
+        d_context, out, act, context_rows, grad_first
+    )
     layer_out = to_parts(out.reshape(count, seq_length, width), parts, hidden.shape)
-    grad_rest = reduce_rows(grad_rest)
+    grad_first = reduce_rows(grad_first)
     d_proj, d_sums = attend_backward(
         proj,
         start,
@@ -494,13 +491,14 @@
         0,
     )
     d_rows = [d_proj[index].reshape(tokens, width) for index in range(3)]
-    stacked = jnp.concatenate([jnp.sum(d_sums, axis=0), sums[:6]], axis=0)
-    stacked = stacked.reshape(8, shards, -1).transpose(1, 0, 2).reshape(shards, -1)
-    sums_up = shards_first(sums_up, shards, blocks)
-    stacked = jnp.concatenate([stacked, sums_up.reshape(shards, -1)], axis=1)
-    stacked = jnp.pad(stacked.reshape(width, -1), ((0, 0), (0, spare))).astype(bf16)
+    stacked = [jnp.sum(d_sums, axis=0), sums[:6], sums_up.reshape(blocks, -1)]
+    stacked = jnp.concatenate(stacked).T.astype(bf16)
     grad_packed = jnp.concatenate(
-        [dot(x_rows, d, TN).astype(bf16) for d in d_rows] + [stacked], axis=1
+        [dot(x_rows, d, TN).astype(bf16) for d in d_rows]
+        + [dot(context_rows, d_attn, TN).astype(bf16)]
+        + [grad_block(act, b) for b in range(later)]
+        + [jnp.pad(stacked, ((0, 0), (0, spare)))],
+        axis=1,
     )
     d_attn, grad_packed = after(d_attn, grad_packed)
     grad_packed = reduce_rows(grad_packed)
@@ -509,15 +507,21 @@
         grad_x = grad_x + dot(d, full_qkv[:, index * width : (index + 1) * width], NT)
     grad_x = grad_x.astype(bf16).reshape(count, seq_length, width)
     grad_hidden = to_parts(grad_x, parts, hidden.shape)
-    grad_rest = reduce_parts(grad_rest, parts)
-    grad_out = grad_rest[:, :width]
-    grad_up = shards_first(grad_rest[:, width:ahead], shards, blocks)
+    grad_first = reduce_parts(grad_first, parts)
+    grad_up = shards_first(grad_first[:, : w_up.shape[1]], shards, blocks)
+    grad_packed = reduce_parts(grad_packed, parts)
+
+    def owned_block(rows, index):
+        return rows[:, index * width : (index + 1) * width]
+
+    grad_out = owned_block(grad_packed, 3)
     grad_down = jnp.concatenate(
-        [grad_rest[:, ahead + b * width : ahead + (b + 1) * width] for b in range(blocks)]
-    )
-    grad_packed = reduce_parts(grad_packed, parts)
-    totals = grad_packed[:, columns : columns + small.shape[1]].reshape(-1)
-    owned = totals[:split].reshape(8, -1)
+        [owned_block(grad_packed, 4 + b) for b in range(later)]
+        + [owned_block(grad_first, b) for b in range(blocks, 2 * blocks - later)]
+    )
+    totals = grad_packed[:, (4 + later) * width :].T
+    owned = totals[:8]
+    grad_bias_up = totals[8 : 8 + blocks].reshape(-1)
     return (
         layer_out,
         grad_hidden,
@@ -529,7 +533,7 @@
         owned[3],
         owned[4],
         grad_up,
-        totals[split:],
+        grad_bias_up,
         grad_down,
         owned[5],
         owned[6],

time: 653 us -> 527 us (0.81)
  waiting for transfers between devices: 281 us -> 177 us
  local copies, waits for them, and re-layouts: 77.2 us -> 58.6 us
    reduce_scatter x2, waiting for transfers between devices: 138 us -> 13.5 us  [reduce_rows(): return lax.psum_scatter(grad, 'shard', scatter_dimension=0, tiled=True)]
    ppermute x2, waiting for transfers between devices: 34.9 us -> 61.6 us  [to_parts(): lax.ppermute(block, 'seq', [(i, (i + shift) % parts) for i in range(parts)])]
    unnamed x52 -> x59, local copies, waits for them, and re-layouts: 17.6 us -> 11.1 us
  transfers between devices with their start and end apart: 11 -> 11, of which waited for: 8 -> 6; matrix products, arithmetic and copies ran while one was open for 12% -> 19% of each run, Pallas kernels for 8% -> 22%
where the time goes in v3:
time: 527 us; the launch traced here: 522 us
  Pallas kernels  184 us (35%)
  waiting for transfers between devices  177 us (34%)
  matrix products  71.5 us (14%)
  local copies, waits for them, and re-layouts  58.6 us (11%)
  between operations  14.5 us (3%)
  other arithmetic  9.89 us (2%)
  starting transfers between devices  7.25 us (1%)
    dot_general x13, matrix products, dot(): return lax.dot_general(a, b, dims, preferred_element_type=f32)  71.5 us
    pallas_call x1, Pallas kernels, middle(): pl.pallas_call(middle_body, grid=(tokens // tile,), in_specs=[rows(width)...  67.3 us
    pallas_call x1, Pallas kernels, attend_backward(): pl.pallas_call(bwd_body, grid_spec=pltpu.PrefetchScalarGridSpec(num_scala...  65.3 us
    ppermute x2, waiting for transfers between devices, to_parts(): lax.ppermute(block, 'seq', [(i, (i + shift) % parts) for i in range(parts)])  61.6 us
    ppermute x3, waiting for transfers between devices, to_whole(): lax.ppermute(block, 'seq', [(i, (i + shift) % parts) for i in range(parts)])  60.6 us
    pallas_call x1, Pallas kernels, attend_forward(): pl.pallas_call(fwd_body, grid_spec=pltpu.PrefetchScalarGridSpec(num_scala...  51.3 us
    all_gather x2, waiting for transfers between devices, gather_rows(): return lax.all_gather(part, 'shard', axis=0, tiled=True)  40 us
    reduce_scatter x2, waiting for transfers between devices, reduce_rows(): return lax.psum_scatter(grad, 'shard', scatter_dimension=0, tiled=True)  13.5 us
  transfers between devices with their start and end apart: 11, of which 6 were waited for; matrix products, arithmetic and copies ran while one was open for 19% of the time, Pallas kernels for 22%

profile of v3, /device:TPU:0, one launch (start us, length us, event | category | flops | bytes accessed | tf_op | source)
XLA Modules:
  0.0 522.5 jit_solution(16874672107381585172)
XLA Ops:
  7.2 0.9 slice_bitcast_fusion.2
  8.1 0.8 stack.35
  9.0 1.6 fusion.37
  10.8 1.7 reshape.80
  12.7 1.4 reshape.81
  14.7 0.7 constant_dynamic-update-slice_fusion
  15.5 1.5 slice_dynamic-update-slice_fusion.3
  17.0 1.5 slice_dynamic-update-slice_fusion.2
  18.5 1.5 slice_dynamic-update-slice_fusion.1
  20.1 1.5 slice_dynamic-update-slice_fusion
  21.6 40.0 %all-gather.3.cloned.1.call-done = bf16[768,2432]{1,0:T(8,128)(2,1)} async-done(((bf16[48,2432]{1,0:T(8,128)(2,1)}), bf16[768,2432]{1,0:T(8,128)(2,1)}) %all-gather.3.cloned.1.call-update) | async-done | bytes 3735568 | tf_op jit(solution)/shard_map/all_gather | solution.py:376
  61.7 2.7 dynamic-slice_bitcast_fusion.3
  64.4 1.5 collective-permute-start
  65.8 1.3 dynamic-slice_bitcast_fusion.2
  67.6 1.5 collective-permute-start.2
  69.3 1.9 bitcast_dynamic-update-slice_fusion.7
  71.2 1.9 broadcast.53.clone.2
  73.1 1.2 bitcast_dynamic-update-slice_fusion.5
  74.4 60.6 %collective-permute-done.2 = s32[2,512]{1,0:T(2,128)S(1)} collective-permute-done((s32[2,512]{1,0:T(2,128)S(1)}, s32[2,512]{1,0:T(2,128)S(1)}, u32[]{:S(2)}, u32[]{:S(2)}) %collective-permute-start.2) | collective-permute-done | bytes 4128 | tf_op jit(solution)/shard_map/ppermute | solution.py:402
  135.4 1.9 broadcast_in_dim_reshape.10.dcol_ref
  138.8 1.6 bitcast_dynamic-update-slice_fusion.6
  140.4 3.8 bitcast_dynamic-update-slice_fusion.4
  145.7 11.8 %add_convert_fusion = bf16[2048,2304]{1,0:T(8,128)(2,1)} fusion(bf16[2048,768]{1,0:T(8,128)(2,1)S(1)} %bitcast.96, f32[2304]{0:T(1024)S(1)} %pad_maximum_fusion.2, bf16[768,2432]{1,0:T(8,128)(2,1)} %all-gather.3.cloned.1.call-done), kind=kOutput, calls=%fused_computation | convolution fusion | flops 7257194496 | bytes 16131072 | tf_op jit(solution)/shard_map/dot_general | solution.py:25
  157.5 51.3 %attend_forward.1 = (bf16[2,1024,768]{2,1,0:T(8,128)(2,1)}, f32[2,6,2,1024]{3,2,1,0:T(2,128)}) custom-call(s32[2,4]{1,0:T(2,128)} %get-tuple-element.69.start_ref, s32[2,4]{1,0:T(2,128)} %get-tuple-element.70.size_ref, bf16[2,1024,2304]{2,1,0:T(8,128)(2,1)} %bitcast.118, bf16[2,1024,2304]{2,1,0:T(8,128)(2,1)} %bitcast.119, bf16[2,1024,2304]{2,1,0:T(8,128)(2,1)} %bitcast.120, ...), custom_call_target="tpu_custom_call" | custom-call | flops 25769803776 | tf_op jit(solution)/shard_map/attend_forward/pallas_call | solution.py:104
  208.8 67.3 %middle.1 = (bf16[2048,768]{1,0:T(8,128)(2,1)}, bf16[2048,768]{1,0:T(8,128)(2,1)}, bf16[2048,768]{1,0:T(8,128)(2,1)}, bf16[2048,768]{1,0:T(8,128)(2,1)}, bf16[20...) custom-call(bf16[2048,768]{1,0:T(8,128)(2,1)} %bitcast.97, ...), custom_call_target="tpu_custom_call" | custom-call | flops 65229815808 | tf_op jit(solution)/shard_map/middle/pallas_call | solution.py:318
  276.1 5.7 %fusion.9 = bf16[768,768]{1,0:T(8,128)(2,1)S(1)} fusion(bf16[2048,768]{1,0:T(8,128)(2,1)} %get-tuple-element.43, bf16[2048,3072]{1,0:T(8,128)(2,1)} %get-tuple-element.50), kind=kOutput, calls=%fused_computation.25 | convolution fusion | flops 2416508928 | bytes 7471104 | tf_op jit(solution)/shard_map/dot_general | solution.py:25
  281.8 5.3 %fusion.12 = bf16[768,768]{1,0:T(8,128)(2,1)S(1)} fusion(bf16[2048,768]{1,0:T(8,128)(2,1)S(1)} %copy-done.18, bf16[2048,3072]{1,0:T(8,128)(2,1)} %get-tuple-element.50), kind=kOutput, calls=%fused_computation.26 | convolution fusion | flops 2416508928 | bytes 7471104 | tf_op jit(solution)/shard_map/dot_general | solution.py:25
  287.1 12.7 %convolution_convert_fusion = bf16[768,3072]{1,0:T(8,128)(2,1)S(1)} fusion(bf16[2048,768]{1,0:T(8,128)(2,1)} %get-tuple-element.41, bf16[2048,3072]{1,0:T(8,128)(2,1)S(1)} %copy-done.20), kind=kOutput, calls=%fused_computation.3 | convolution fusion | flops 9666035712 | bytes 20447232 | tf_op jit(solution)/shard_map/dot_general | solution.py:25
  299.8 3.3 pad_maximum_fusion
  303.2 65.3 %attend_backward.1 = (bf16[3,2,1024,768]{3,2,1,0:T(8,128)(2,1)}, f32[2,2,768]{2,1,0:T(2,128)}) custom-call(s32[2,4]{1,0:T(2,128)} %get-tuple-element.69.start_ref, s32[2,4]{1,0:T(2,128)} %get-tuple-element.70.size_ref, bf16[2,1024,2304]{2,1,0:T(8,128)(2,1)} %bitcast.121, bf16[2,1024,2304]{2,1,0:T(8,128)(2,1)} %bitcast.122, bf16[2,1024,2304]{2,1,0:T(8,128)(2,1)} %bitcast.123, ...), custom_call_target="tpu_custom_call" | custom-call | flops 38654705664 | tf_op jit(solution)/shard_map/attend_backward/pallas_call | solution.py:194
  369.5 4.4 fusion.39
  374.2 3.9 fusion.30
  378.1 3.8 fusion.29
  381.9 3.8 fusion.28
  385.7 3.9 fusion.27
  389.6 4.1 fusion.18
  393.7 3.9 fusion.24
  397.6 0.7 pad_dynamic-update-slice_fusion
  398.3 5.1 fusion.34
  403.5 2.7 fusion.32
  406.2 4.9 add_convert_fusion.1
  411.1 1.3 dynamic-slice_bitcast_fusion
  412.4 1.2 copy-done.10
  413.5 1.2 dynamic-slice_bitcast_fusion.1
  414.8 0.9 collective-permute-start.3
  416.1 1.7 copy-done.5
  418.1 1.2 collective-permute-start.6
  419.4 30.6 %collective-permute-done.4 = bf16[2,512,768]{2,1,0:T(8,128)(2,1)} collective-permute-done((bf16[2,512,768]{2,1,0:T(8,128)(2,1)}, bf16[2,512,768]{2,1,0:T(8,128)(2,1)}, u32[]{:S(2)}, u32[]{:S(2)}) %collective-permute-start.4) | collective-permute-done | bytes 1572896 | tf_op jit(solution)/shard_map/ppermute | solution.py:415
  449.9 2.7 bitcast_dynamic-update-slice_fusion
  452.6 31.1 %collective-permute-done.3 = bf16[2,512,768]{2,1,0:T(8,128)(2,1)} collective-permute-done((bf16[2,512,768]{2,1,0:T(8,128)(2,1)}, bf16[2,512,768]{2,1,0:T(8,128)(2,1)}, u32[]{:S(2)}, u32[]{:S(2)}) %collective-permute-start.3) | collective-permute-done | bytes 1572896 | tf_op jit(solution)/shard_map/ppermute | solution.py:415
  483.7 1.6 bitcast_dynamic-update-slice_fusion.2
  485.3 13.5 %reduce-scatter.3.cloned.1.call-done = bf16[48,4736]{1,0:T(8,128)(2,1)} async-done(((bf16[768,4736]{1,0:T(8,128)(2,1)}), bf16[48,4736]{1,0:T(8,128)(2,1)}) %reduce-scatter.3.cloned.1.call-update) | async-done | bytes 454672 | tf_op jit(solution)/shard_map/reduce_scatter | solution.py:380
  498.7 1.5 collective-permute-start.5
  500.2 1.2 convert_add_fusion.1
  501.5 0.9 copy-done
  502.4 0.9 slice.195
  503.2 1.7 reshape.87
  505.7 2.6 reshape.88
  508.3 1.0 fusion.41
  509.3 1.1 collective-permute-done.5
  510.4 1.2 convert_add_fusion
  512.4 0.8 slice.187
  513.2 0.8 slice_reduce_fusion
  514.8 0.9 pad_maximum_fusion.1
  (103 shorter events, 9.6 us)
Async XLA Ops:
  7.2 6.9 %copy-start.12 = (bf16[48,768]{1,0:T(8,128)(2,1)S(1)}, bf16[48,768]{1,0:T(8,128)(2,1)}, u32[]{:S(2)}) copy-start(bf16[48,768]{1,0:T(8,128)(2,1)} %param.22) | copy-start | bytes 221188
  7.2 54.4 %all-gather.3.cloned.1.call-start = ((), (), s32[]{:S(2)}) async-start(), calls=%async_computation.2 | async-start | bytes 3969024 | tf_op jit(solution)/shard_map/all_gather | solution.py:376
  10.7 198.1 %all-gather.5.cloned.1.call-start = ((), (), s32[]{:S(2)}) async-start(), calls=%async_computation.3 | async-start | bytes 11280384 | tf_op jit(solution)/shard_map/all_gather | solution.py:376
  14.1 51.8 %copy-start.8 = (bf16[2,2,512,768]{3,2,1,0:T(8,128)(2,1)S(1)}, bf16[2,2,512,768]{3,2,1,0:T(8,128)(2,1)}, u32[]{:S(2)}) copy-start(bf16[2,2,512,768]{3,2,1,0:T(8,128)(2,1)} %param.17) | copy-start | bytes 9437188
  61.6 356.5 %reduce-scatter.5.cloned.1.call-start = ((), (), s32[]{:S(2)}) async-start(), calls=%async_computation.5 | async-start | bytes 7520256 | tf_op jit(solution)/shard_map/reduce_scatter | solution.py:380
  61.7 6.0 %copy-start.14 = (s32[2,2,512]{2,1,0:T(2,128)S(1)}, s32[2,2,512]{2,1,0:T(2,128)}, u32[]{:S(2)}) copy-start(s32[2,2,512]{2,1,0:T(2,128)} %param.18) | copy-start | bytes 24580
  64.4 74.4 %collective-permute-start = (bf16[2,512,768]{2,1,0:T(8,128)(2,1)}, bf16[2,512,768]{2,1,0:T(8,128)(2,1)}, u32[]{:S(2)}, u32[]{:S(2)}) collective-permute-start(bf16[2,512,768]{2,1,0:T(8,128)(2,1)} %dynamic-slice_bitcast_fusion.3), channel_id=1, source_target_pairs={{0,16},{16,0},{1,17},{17,1},{2,18},{18,2},{3,19},{19,3},{4,20},{20... | collective-permute-start | bytes 4718600 | tf_op jit(solution)/shard_map/ppermute | solution.py:402
  67.1 73.3 %collective-permute-start.1 = (bf16[2,512,768]{2,1,0:T(8,128)(2,1)}, bf16[2,512,768]{2,1,0:T(8,128)(2,1)}, u32[]{:S(2)}, u32[]{:S(2)}) collective-permute-start(bf16[2,512,768]{2,1,0:T(8,128)(2,1)} %dynamic-slice_bitcast_fusion.2), channel_id=1, source_target_pairs={{0,16},{16,0},{1,17},{17,1},{2,18},{18,2},{3,19},{19,3},{4,20},{20... | collective-permute-start | bytes 4718600 | tf_op jit(solution)/shard_map/ppermute | solution.py:402
  67.6 67.3 %collective-permute-start.2 = (s32[2,512]{1,0:T(2,128)S(1)}, s32[2,512]{1,0:T(2,128)S(1)}, u32[]{:S(2)}, u32[]{:S(2)}) collective-permute-start(s32[2,512]{1,0:T(2,128)S(1)} %get-tuple-element.79), channel_id=1, source_target_pairs={{0,16},{16,0},{1,17},{17,1},{2,18},{18,2},{3,19},{19,3},{4,20},{20... | collective-permute-start | bytes 12296 | tf_op jit(solution)/shard_map/ppermute | solution.py:402
  69.3 3.8 copy-start.9
  138.8 5.5 %slice-start = ((bf16[768,2432]{1,0:T(8,128)(2,1)}), bf16[768,128]{1,0:T(8,128)(2,1)S(1)}, s32[]{:S(2)}) async-start(bf16[768,2432]{1,0:T(8,128)(2,1)} %all-gather.3.cloned.1.call-done), calls=%async_computation.6 | async-start | bytes 393216 | tf_op jit(solution)/shard_map/slice | solution.py:441
  140.4 17.1 %copy-start.6 = (bf16[2,2,512,768]{3,2,1,0:T(8,128)(2,1)}, bf16[2,2,512,768]{3,2,1,0:T(8,128)(2,1)S(1)}, u32[]{:S(2)}) copy-start(bf16[2,2,512,768]{3,2,1,0:T(8,128)(2,1)S(1)} %bitcast_dynamic-update-slice_fusion.6) | copy-start | bytes 9437188
  276.1 5.7 %copy-start.18 = (bf16[2048,768]{1,0:T(8,128)(2,1)S(1)}, bf16[2048,768]{1,0:T(8,128)(2,1)}, u32[]{:S(2)}) copy-start(bf16[2048,768]{1,0:T(8,128)(2,1)} %get-tuple-element.43) | copy-start | bytes 9437188
  276.1 11.0 %copy-start.20 = (bf16[2048,3072]{1,0:T(8,128)(2,1)S(1)}, bf16[2048,3072]{1,0:T(8,128)(2,1)}, u32[]{:S(2)}) copy-start(bf16[2048,3072]{1,0:T(8,128)(2,1)} %get-tuple-element.42) | copy-start | bytes 37748740
  303.1 195.6 %reduce-scatter.3.cloned.1.call-start = ((), (), s32[]{:S(2)}) async-start(), calls=%async_computation.4 | async-start | bytes 7729152 | tf_op jit(solution)/shard_map/reduce_scatter | solution.py:380
  303.1 66.1 %copy-start.13 = (f32[1,3072]{1,0:T(1,128)S(1)}, f32[1,3072]{1,0:T(1,128)}, u32[]{:S(2)}) copy-start(f32[1,3072]{1,0:T(1,128)} %get-tuple-element.53) | copy-start | bytes 36868
  303.2 66.1 %copy-start.15 = (f32[8,768]{1,0:T(8,128)S(1)}, f32[8,768]{1,0:T(8,128)}, u32[]{:S(2)}) copy-start(f32[8,768]{1,0:T(8,128)} %get-tuple-element.52) | copy-start | bytes 73732
  369.5 4.7 copy-start.7
  374.0 4.2 copy-start.3
  374.0 4.1 copy-start.1
  374.2 15.3 %slice-start.1 = ((s8[12582912]{0:T(1024)(128)(4,1)}), s8[4194304]{0:T(1024)(128)(4,1)S(1)}, s32[]{:S(2)}) async-start(s8[12582912]{0:T(1024)(128)(4,1)} %bitcast.127), calls=%async_computation.7 | async-start | bytes 8388608
  378.1 11.4 %slice-start.2 = ((s8[12582912]{0:T(1024)(128)(4,1)}), s8[4194304]{0:T(1024)(128)(4,1)S(1)}, s32[]{:S(2)}) async-start(s8[12582912]{0:T(1024)(128)(4,1)} %bitcast.127), calls=%async_computation.8 | async-start | bytes 8388608
  381.9 3.8 copy-start.16
  381.9 3.8 copy-start.17
  381.9 7.6 %slice-start.3 = ((s8[12582912]{0:T(1024)(128)(4,1)}), s8[4194304]{0:T(1024)(128)(4,1)S(1)}, s32[]{:S(2)}) async-start(s8[12582912]{0:T(1024)(128)(4,1)} %bitcast.127), calls=%async_computation.9 | async-start | bytes 8388608
  385.7 3.9 copy-start.19
  398.3 5.1 copy-start.2
  398.3 5.1 copy-start.11
  411.1 2.5 copy-start.10
  412.4 37.6 %collective-permute-start.4 = (bf16[2,512,768]{2,1,0:T(8,128)(2,1)}, bf16[2,512,768]{2,1,0:T(8,128)(2,1)}, u32[]{:S(2)}, u32[]{:S(2)}) collective-permute-start(bf16[2,512,768]{2,1,0:T(8,128)(2,1)} %dynamic-slice_bitcast_fusion), channel_id=1, source_target_pairs={{0,16},{16,0},{1,17},{17,1},{2,18},{18,2},{3,19},{19,3},{4,20},{20... | collective-permute-start | bytes 4718600 | tf_op jit(solution)/shard_map/ppermute | solution.py:415
  414.8 68.9 %collective-permute-start.3 = (bf16[2,512,768]{2,1,0:T(8,128)(2,1)}, bf16[2,512,768]{2,1,0:T(8,128)(2,1)}, u32[]{:S(2)}, u32[]{:S(2)}) collective-permute-start(bf16[2,512,768]{2,1,0:T(8,128)(2,1)} %dynamic-slice_bitcast_fusion.1), channel_id=1, source_target_pairs={{0,16},{16,0},{1,17},{17,1},{2,18},{18,2},{3,19},{19,3},{4,20},{20... | collective-permute-start | bytes 4718600 | tf_op jit(solution)/shard_map/ppermute | solution.py:415
  416.0 1.7 copy-start.5
  418.1 82.1 %collective-permute-start.6 = (bf16[48,4608]{1,0:T(8,128)(2,1)}, bf16[48,4608]{1,0:T(8,128)(2,1)}, u32[]{:S(2)}, u32[]{:S(2)}) collective-permute-start(bf16[48,4608]{1,0:T(8,128)(2,1)} %reduce-scatter.5.cloned.1.call-done), channel_id=1, source_target_pairs={{0,16},{16,0},{1,17},{17,1},{2,18},{18,2},{3,19},{19,3},{4,20},{20... | collective-permute-start | bytes 1327112 | tf_op jit(solution)/shard_map/ppermute | solution.py:363
  485.2 16.2 %copy-start.4 = (bf16[2,2,512,768]{3,2,1,0:T(8,128)(2,1)}, bf16[2,2,512,768]{3,2,1,0:T(8,128)(2,1)S(1)}, u32[]{:S(2)}) copy-start(bf16[2,2,512,768]{3,2,1,0:T(8,128)(2,1)S(1)} %bitcast_dynamic-update-slice_fusion.2) | copy-start | bytes 9437188
  498.7 11.7 %collective-permute-start.5 = (bf16[48,4736]{1,0:T(8,128)(2,1)}, bf16[48,4736]{1,0:T(8,128)(2,1)}, u32[]{:S(2)}, u32[]{:S(2)}) collective-permute-start(bf16[48,4736]{1,0:T(8,128)(2,1)} %reduce-scatter.3.cloned.1.call-done), channel_id=1, source_target_pairs={{0,16},{16,0},{1,17},{17,1},{2,18},{18,2},{3,19},{19,3},{4,20},{20... | collective-permute-start | bytes 1363976 | tf_op jit(solution)/shard_map/ppermute | solution.py:363
  501.5 0.9 copy-start
Sparse Core Ops, SparseCore 0:
  10.8 50.7 all-gather.2
  63.9 87.0 all-gather.4
  303.2 93.1 reduce-scatter.4
  400.3 98.3 reduce-scatter.2
